TPU v7x, 32 devices: a whole 2x2x4 slice. The times are simulated.
32 devices in a mesh: dp: 16 (over z, y, core), seq: 2 (over x).
Axes of the slice: x: 2, y: 2, z: 4, core: 2. Of those that a mesh axis runs over, the one named last changes fastest.
Arguments:
- tokens: bfloat16 [16384, 768], P(('dp', 'seq')), may hold values from -6 to 6
- lengths: int32 [16, 6], P('dp'), may hold values from 1 to 768, 1024 in all within a row
- w_qkv: bfloat16 [768, 2304], P('dp'), may hold values from -0.21875 to 0.21875
- w_out: bfloat16 [768, 768], P('dp'), may hold values from -2.5 to 2.5
- w_up: bfloat16 [768, 3072], P('dp'), may hold values from -0.21875 to 0.21875
- w_down: bfloat16 [3072, 768], P('dp'), may hold values from -0.109375 to 0.109375
- bias_q: bfloat16 [768], P('dp'), may hold values from -4 to 4
- bias_v: bfloat16 [768], P('dp'), may hold values from -4 to 4
- bias_out: bfloat16 [768], P('dp'), may hold values from -4 to 4
- bias_up: bfloat16 [3072], P('dp'), may hold values from -4 to 4
- bias_down: bfloat16 [768], P('dp'), may hold values from -4 to 4
- gain_one: bfloat16 [768], P('dp'), may hold values from 0.5 to 1.5
- shift_one: bfloat16 [768], P('dp'), may hold values from -4 to 4
- gain_two: bfloat16 [768], P('dp'), may hold values from 0.5 to 1.5
- shift_two: bfloat16 [768], P('dp'), may hold values from -4 to 4
- cotangent: bfloat16 [16384, 768], P(('dp', 'seq')), may hold values from -6 to 6
Outputs:
- block_out: bfloat16 [16384, 768], P(('dp', 'seq'))
- grad_tokens: float32 [16384, 768], P(('dp', 'seq'))
- grad_w_qkv: float32 [768, 2304], P('dp')
- grad_w_out: float32 [768, 768], P('dp')
- grad_w_up: float32 [768, 3072], P('dp')
- grad_w_down: float32 [3072, 768], P('dp')
- grad_bias_q: float32 [768], P('dp')
- grad_bias_v: float32 [768], P('dp')
- grad_bias_out: float32 [768], P('dp')
- grad_bias_up: float32 [3072], P('dp')
- grad_bias_down: float32 [768], P('dp')
- grad_gain_one: float32 [768], P('dp')
- grad_shift_one: float32 [768], P('dp')
- grad_gain_two: float32 [768], P('dp')
- grad_shift_two: float32 [768], P('dp')
Inputs may be any that keep to these rules, and one draw needn't show every extreme that they name: Row g holds the lengths of the 6 slots that fill the 1024 positions of group g in order; the last slot is padding; the longest slot of each row has exactly 768 positions.
All inputs are finite; a program needn't handle non-finite values.
Results may differ from a plain program's by a relative error of at most 0.011.
Values may be sent and summed in bfloat16 or wider, within the bound.
A program may use at most 192 MiB of HBM per device.

v0:
```python
import jax
import jax.numpy as jnp
from jax import lax
from jax.sharding import PartitionSpec as P

HEAD_DIM = 64


EPSILON = 1e-05
MASKED = -1e30
SLOPE = 0.7978845608028654
CUBIC = 0.044715


def as_sent(array):
    return jax.tree.map(lambda a: a.astype(jnp.bfloat16) if a.dtype == jnp.float32 else a, array)


def dense(left, right):
    return jnp.dot(left, right, preferred_element_type=jnp.float32)


def dense_left(left, right):
    return lax.dot_general(
        left, right, (((0,), (0,)), ((), ())), preferred_element_type=jnp.float32
    )


def dense_right(left, right):
    return lax.dot_general(
        left, right, (((1,), (1,)), ((), ())), preferred_element_type=jnp.float32
    )


def norm_parts(value):
    mean = jnp.mean(value, axis=-1, keepdims=True)
    centred = value - mean
    inverse = lax.rsqrt(jnp.mean(centred * centred, axis=-1, keepdims=True) + EPSILON)
    return (centred * inverse, inverse)


def norm_back(grad, scaled, inverse, gain):
    shaped = grad * gain
    inner = jnp.mean(shaped * scaled, axis=-1, keepdims=True)
    return inverse * (shaped - jnp.mean(shaped, axis=-1, keepdims=True) - scaled * inner)


def gelu_value(value):
    return 0.5 * value * (1.0 + jnp.tanh(SLOPE * (value + CUBIC * value * value * value)))


def gelu_slope(value):
    bent = jnp.tanh(SLOPE * (value + CUBIC * value * value * value))
    return 0.5 * (1.0 + bent) + 0.5 * value * (1.0 - bent * bent) * SLOPE * (
        1.0 + 3.0 * CUBIC * value * value
    )


def per_device(
    tokens,
    lengths,
    w_qkv,
    w_out,
    w_up,
    w_down,
    bias_q,
    bias_v,
    bias_out,
    bias_up,
    bias_down,
    gain_one,
    shift_one,
    gain_two,
    shift_two,
    cotangent,
):
    width = tokens.shape[1]
    rows = tokens.shape[0]
    pair = lax.axis_size("seq")
    rank = lax.axis_index("seq")
    group = rows * pair
    local = width // pair
    heads = local // HEAD_DIM
    scale = HEAD_DIM ** (-0.5)
    block = 512
    blocks = group // block
    whole = (
        lax.all_gather(w_qkv, "dp", axis=0, tiled=True),
        lax.all_gather(w_out, "dp", axis=0, tiled=True),
        lax.all_gather(w_up, "dp", axis=0, tiled=True),
        lax.all_gather(w_down, "dp", axis=0, tiled=True),
        lax.all_gather(bias_q, "dp", axis=0, tiled=True),
        lax.all_gather(bias_v, "dp", axis=0, tiled=True),
        lax.all_gather(bias_out, "dp", axis=0, tiled=True),
        lax.all_gather(bias_up, "dp", axis=0, tiled=True),
        lax.all_gather(bias_down, "dp", axis=0, tiled=True),
        lax.all_gather(gain_one, "dp", axis=0, tiled=True),
        lax.all_gather(shift_one, "dp", axis=0, tiled=True),
        lax.all_gather(gain_two, "dp", axis=0, tiled=True),
        lax.all_gather(shift_two, "dp", axis=0, tiled=True),
    )
    weight_qkv, weight_out, weight_up, weight_down = whole[0:4]
    add_q, add_v, add_out, add_up, add_down, scale_one, move_one, scale_two, move_two = [
        piece.astype(jnp.float32) for piece in whole[4:]
    ]
    slots = lengths.shape[1]
    position = jnp.arange(group, dtype=jnp.int32)
    ends = jnp.cumsum(lengths[0])
    segment = jnp.sum((position[:, None] >= ends[None, :]).astype(jnp.int32), axis=1)
    own_segment = lax.dynamic_slice_in_dim(segment, rank * rows, rows)
    valid = (own_segment < slots - 1)[:, None]
    inputs = tokens.astype(jnp.float32)
    scaled_one, inverse_one = norm_parts(inputs)
    first = (scaled_one * scale_one + move_one).astype(jnp.bfloat16)
    bias_qkv = jnp.concatenate([add_q, jnp.zeros_like(add_q), add_v])
    qkv = (dense(first, weight_qkv) + bias_qkv).astype(jnp.bfloat16)
    head_side = lax.all_to_all(
        qkv.reshape(rows, 3, pair, local), "seq", split_axis=2, concat_axis=0, tiled=True
    )
    query = head_side[:, 0, 0].reshape(group, heads, HEAD_DIM)
    keys = head_side[:, 1, 0].reshape(group, heads, HEAD_DIM)
    values = head_side[:, 2, 0].reshape(group, heads, HEAD_DIM)

    def block_scores(index):
        start = index * block
        query_rows = lax.dynamic_slice_in_dim(query, start, block)
        raw = (
            jnp.einsum("qhd,khd->hqk", query_rows, keys, preferred_element_type=jnp.float32) * scale
        )
        row_segment = lax.dynamic_slice_in_dim(segment, start, block)
        row_position = lax.dynamic_slice_in_dim(position, start, block)
        allowed = (row_segment[:, None] == segment[None, :]) & (
            position[None, :] <= row_position[:, None]
        )
        return (jnp.where(allowed[None], raw, MASKED), query_rows)

    def attend(index):
        scores, unused = block_scores(index)
        top = jnp.max(scores, axis=-1, keepdims=True)
        weights = jnp.exp(scores - top)
        total = jnp.sum(weights, axis=-1, keepdims=True)
        probs = (weights / total).astype(jnp.bfloat16)
        mixed_rows = jnp.einsum("hqk,khd->qhd", probs, values, preferred_element_type=jnp.float32)
        return (
            mixed_rows.reshape(block, local).astype(jnp.bfloat16),
            (top + jnp.log(total))[:, :, 0],
        )

    mixed_blocks, log_totals = lax.map(attend, jnp.arange(blocks))
    mixed_head = mixed_blocks.reshape(group, 1, local)
    mixed = lax.all_to_all(mixed_head, "seq", split_axis=0, concat_axis=1, tiled=True).reshape(
        rows, width
    )
    middle = inputs + dense(mixed, weight_out) + add_out
    scaled_two, inverse_two = norm_parts(middle)
    second = (scaled_two * scale_two + move_two).astype(jnp.bfloat16)
    pre = dense(second, weight_up) + add_up
    hidden = gelu_value(pre).astype(jnp.bfloat16)
    result = middle + dense(hidden, weight_down) + add_down
    block_out = jnp.where(valid, result, 0.0).astype(jnp.bfloat16)
    grad_out = jnp.where(valid, cotangent, jnp.zeros_like(cotangent))
    grad_weight_down = dense_left(hidden, grad_out)
    grad_add_down = jnp.sum(grad_out.astype(jnp.float32), axis=0)
    grad_pre = (dense_right(grad_out, weight_down) * gelu_slope(pre)).astype(jnp.bfloat16)
    grad_weight_up = dense_left(second, grad_pre)
    grad_add_up = jnp.sum(grad_pre.astype(jnp.float32), axis=0)
    grad_second = dense_right(grad_pre, weight_up)
    grad_scale_two = jnp.sum(grad_second * scaled_two, axis=0)
    grad_move_two = jnp.sum(grad_second, axis=0)
    grad_middle = grad_out.astype(jnp.float32) + norm_back(
        grad_second, scaled_two, inverse_two, scale_two
    )
    grad_attn = grad_middle.astype(jnp.bfloat16)
    grad_weight_out = dense_left(mixed, grad_attn)
    grad_add_out = jnp.sum(grad_attn.astype(jnp.float32), axis=0)
    grad_mixed = dense_right(grad_attn, weight_out).astype(jnp.bfloat16)
    branch_grads = (
        grad_weight_out,
        grad_weight_up,
        grad_weight_down,
        grad_add_out,
        grad_add_up,
        grad_add_down,
        grad_scale_two,
        grad_move_two,
    )
    grad_head = lax.all_to_all(
        grad_mixed.reshape(rows, pair, local), "seq", split_axis=1, concat_axis=0, tiled=True
    )
    grad_head = grad_head.reshape(group, heads, HEAD_DIM)

    def attend_back(carry, index):
        grad_keys, grad_values = carry
        scores, query_rows = block_scores(index)
        probs = jnp.exp(scores - log_totals[index][:, :, None])
        grad_rows = lax.dynamic_slice_in_dim(grad_head, index * block, block)
        grad_probs = jnp.einsum(
            "qhd,khd->hqk", grad_rows, values, preferred_element_type=jnp.float32
        )
        centre = jnp.sum(probs * grad_probs, axis=-1, keepdims=True)
        grad_scores = (probs * (grad_probs - centre)).astype(jnp.bfloat16)
        grad_values = grad_values + jnp.einsum(
            "hqk,qhd->khd",
            probs.astype(jnp.bfloat16),
            grad_rows,
            preferred_element_type=jnp.float32,
        )
        grad_keys = (
            grad_keys
            + jnp.einsum(
                "hqk,qhd->khd", grad_scores, query_rows, preferred_element_type=jnp.float32
            )
            * scale
        )
        grad_query = (
            jnp.einsum("hqk,khd->qhd", grad_scores, keys, preferred_element_type=jnp.float32)
            * scale
        )
        return ((grad_keys, grad_values), grad_query)

    empty = jnp.zeros((group, heads, HEAD_DIM), jnp.float32)
    (grad_keys, grad_values), grad_queries = lax.scan(
        attend_back, (empty, empty), jnp.arange(blocks)
    )
    grad_side = jnp.stack(
        [
            grad_queries.reshape(group, local),
            grad_keys.reshape(group, local),
            grad_values.reshape(group, local),
        ],
        axis=1,
    ).astype(jnp.bfloat16)
    grad_qkv = lax.all_to_all(
        grad_side.reshape(group, 3, 1, local), "seq", split_axis=0, concat_axis=2, tiled=True
    )
    grad_qkv = grad_qkv.reshape(rows, 3 * width)
    grad_weight_qkv = dense_left(first, grad_qkv)
    column_sums = jnp.sum(grad_qkv.astype(jnp.float32), axis=0)
    grad_add_q = column_sums[:width]
    grad_add_v = column_sums[2 * width :]
    grad_first = dense_right(grad_qkv, weight_qkv)
    grad_scale_one = jnp.sum(grad_first * scaled_one, axis=0)
    grad_move_one = jnp.sum(grad_first, axis=0)
    grad_tokens = grad_middle + norm_back(grad_first, scaled_one, inverse_one, scale_one)
    stem_grads = (grad_weight_qkv, grad_add_q, grad_add_v, grad_scale_one, grad_move_one)
    halves = lax.psum_scatter(
        stem_grads + branch_grads, ("dp", "seq"), scatter_dimension=0, tiled=True
    )
    shares = jax.tree.map(
        lambda part, own: part.astype(own.dtype),
        lax.all_gather(as_sent(halves), "seq", axis=0, tiled=True),
        halves,
    )
    stem_shares = shares[0:5]
    branch_shares = shares[5:13]
    return (
        block_out,
        grad_tokens,
        stem_shares[0],
        branch_shares[0],
        branch_shares[1],
        branch_shares[2],
        stem_shares[1],
        stem_shares[2],
        branch_shares[3],
        branch_shares[4],
        branch_shares[5],
        stem_shares[3],
        stem_shares[4],
        branch_shares[6],
        branch_shares[7],
    )


def solution(mesh):
    return jax.shard_map(
        per_device,
        mesh=mesh,
        in_specs=(
            P(("dp", "seq"), None),
            P("dp", None),
            P("dp", None),
            P("dp", None),
            P("dp", None),
            P("dp", None),
            P("dp"),
            P("dp"),
            P("dp"),
            P("dp"),
            P("dp"),
            P("dp"),
            P("dp"),
            P("dp"),
            P("dp"),
            P(("dp", "seq"), None),
        ),
        out_specs=(
            P(("dp", "seq"), None),
            P(("dp", "seq"), None),
            P("dp", None),
            P("dp", None),
            P("dp", None),
            P("dp", None),
            P("dp"),
            P("dp"),
            P("dp"),
            P("dp"),
            P("dp"),
            P("dp"),
            P("dp"),
            P("dp"),
            P("dp"),
        ),
        check_vma=False,
    )
```

profile of v0, /device:TPU:0, one launch (start us, length us, event | category | flops | bytes accessed | tf_op | source)
XLA Modules:
  0.0 803.9 jit_solution(13728471916678180255)
XLA Ops:
  19.5 63.7 %all-reduce.28 = (bf16[768]{0:T(1024)(128)(2,1)S(1)}, bf16[768]{0:T(1024)(128)(2,1)S(1)}, bf16[768]{0:T(1024)(128)(2,1)S(1)}, bf16[768]{0:T(1024)(128)(2,1)S(1)}...) all-reduce(bf16[768]{0:T(1024)(128)(2,1)S(1)} %dynamic-update-slice, ...), channel_id=1, replica_groups=mesh['dp'=16,'seq'=2] {'dp'}, use_global_device_ids=true, to_apply=%add.3 | all-reduce | flops 9216 | bytes 36864
  86.7 5.8 fusion.36
  92.6 4.6 reshape.329
  98.9 3.9 all-to-all-start
  103.7 22.7 %all-to-all-done = bf16[512,3,2,384]{3,0,1,2:T(8,128)(2,1)S(1)} async-done(((bf16[512,3,2,384]{3,0,1,2:T(8,128)(2,1)}), bf16[512,3,2,384]{3,0,1,2:T(8,128)(2,1)S(1)}, u32[]{:S(2)}, u32[]{:S(2)}) %all-to-all-start) | async-done | bytes 2359328 | tf_op jit(solution)/shard_map/all_to_all | solution.py:117
  130.1 26.7 %while.29 = (s32[]{:T(128)}, bf16[2,512,384]{2,1,0:T(8,128)(2,1)}, f32[2,6,512]{2,1,0:T(8,128)S(1)}, s32[2]{0:T(128)S(1)}, s32[1024]{0:T(1024)S(1)}, /*index=5*/...) while((s32[]{:T(128)}, bf16[2,512,384]{2,1,0:T(8,128)(2,1)}, ...), condition=%wide.region_7.8_spmd.clone, body=%wide.region_4.7_spmd.clone.sunk | while | flops 844821504 | bytes 43909328 | solution.py:149
  134.4 3.6 fusion.104
  138.0 4.3 fusion.105
  147.7 3.6 fusion.104
  151.4 4.3 fusion.105
  162.2 4.7 all-to-all-start.1
  167.1 7.9 all-to-all-done.1
  182.3 3.2 fusion.63
  187.0 8.2 %fusion.60 = f32[512,3072]{1,0:T(8,128)} fusion(bf16[768,3072]{1,0:T(8,128)(2,1)} %all-gather.9.cloned.1.call-done, f32[512,768]{1,0:T(8,128)} %copy-done.7, f32[768]{0:T(1024)S(1)} %convert_element_type.192, f32[768]{0:T(1024)S(1)} %convert_element_type.191, f32[512]{0:T(512)S(1)} %add_rsqrt_fusion, f32[512]{0:T(512)S(1)} %broadcast_multiply_fusion.4), kind=kOutput, calls=%fused_computation.114 | convolution fusion | flops 2417885184 | bytes 12593152 | tf_op jit(solution)/shard_map/dot_general | solution.py:20
  195.2 13.9 %all-gather.11.cloned.1.call-done = bf16[3072,768]{1,0:T(8,128)(2,1)} async-done(((bf16[192,768]{1,0:T(8,128)(2,1)}), bf16[3072,768]{1,0:T(8,128)(2,1)}) %all-gather.11.cloned.1.call-update) | async-done | bytes 4718608 | tf_op jit(solution)/shard_map/all_gather | solution.py:91
  209.1 9.7 %convert_reduce_fusion = (f32[3072]{0:T(1024)}, bf16[512,3072]{1,0:T(8,128)(2,1)S(1)}) fusion(f32[512,3072]{1,0:T(8,128)} %fusion.60, f32[3072]{0:T(1024)S(1)} %convert_element_type.194, bf16[3072,768]{1,0:T(8,128)(2,1)} %all-gather.11.cloned.1.call-done, bf16[512,768]{1,0:T(8,128)(2,1)} %param.35, pred[512]{0:T(512)(128)(4,1)S(1)} %dynamic-slice_compare_fusion), kind=kOutput, calls=%fused_computation.49 | convolution fusion | flops 2450912256 | bytes 14967296 | tf_op jit(solution)/shard_map/dot_general | solution.py:30
  218.8 3.6 multiply_reduce_fusion.1
  226.9 4.3 all-to-all-start.2
  231.3 3.8 fusion.52
  235.2 7.6 all-to-all-done.2
  245.8 3.2 reshape.333
  249.1 81.8 %while.30 = (s32[]{:T(128)}, f32[1024,6,64]{0,2,1:T(8,128)}, f32[1024,6,64]{0,2,1:T(8,128)}, bf16[2,512,6,64]{1,3,2,0:T(8,128)(2,1)}, s32[2]{0:T(128)S(1)}, /*in...) while((s32[]{:T(128)}, f32[1024,6,64]{0,2,1:T(8,128)}, ...), condition=%wide.region_14.15_spmd.clone.clone, body=%wide.region_12.14_spmd.clone.clone.sunk | while | flops 2064184320 | bytes 227123792 | solution.py:222
  250.6 6.4 fusion.115
  259.6 7.8 multiply_reduce_fusion.7
  268.6 5.0 multiply_convert_fusion.5
  273.6 5.4 bitcast_add_fusion.4
  280.6 6.0 bitcast_add_fusion.5
  290.8 6.4 fusion.115
  299.9 7.7 multiply_reduce_fusion.7
  308.6 5.0 multiply_convert_fusion.5
  313.7 5.8 bitcast_add_fusion.4
  321.1 6.6 bitcast_add_fusion.5
  336.0 4.9 copy.104
  340.9 38.6 %all_to_all.63 = bf16[1024,3,1,384]{3,1,2,0:T(4,128)(2,1)S(1)} all-to-all(bf16[1024,3,1,384]{3,1,2,0:T(4,128)(2,1)S(1)} %copy.104), channel_id=1, replica_groups=mesh['dp'=16,'seq'=2] {'seq'}, dimensions={0} | all-to-all | bytes 4718592 | tf_op jit(solution)/shard_map/all_to_all | solution.py:233
  382.3 6.9 fusion.55
  389.9 8.9 %fusion.59 = f32[768,3072]{1,0:T(8,128)} fusion(bf16[512,3072]{1,0:T(8,128)(2,1)} %copy-done.43, f32[512,768]{1,0:T(8,128)} %copy-done.7, f32[768]{0:T(1024)S(1)} %copy-done.33, f32[768]{0:T(1024)S(1)} %copy-done.20, f32[512]{0:T(512)S(1)} %copy-done.27, f32[512]{0:T(512)S(1)} %copy-done.14), kind=kOutput, calls=%fused_computation.113 | convolution fusion | flops 2417885184 | bytes 14166016 | tf_op jit(solution)/shard_map/dot_general | solution.py:24
  399.5 10.4 %fusion.58 = f32[3072,768]{1,0:T(8,128)} fusion(bf16[512,768]{1,0:T(8,128)(2,1)} %param.35, pred[512]{0:T(512)(128)(4,1)S(1)} %copy-done.37, f32[512,3072]{1,0:T(8,128)} %fusion.60, f32[3072]{0:T(1024)S(1)} %copy-done.24), kind=kOutput, calls=%fused_computation.112 | convolution fusion | flops 2432040960 | bytes 16527872 | tf_op jit(solution)/shard_map/dot_general | solution.py:24
  412.5 9.9 %select_convert_fusion = bf16[512,768]{1,0:T(8,128)(2,1)} fusion(f32[512,768]{1,0:T(8,128)} %copy-done.7, bf16[3072,768]{1,0:T(8,128)(2,1)} %all-gather.11.cloned.1.call-done, f32[768]{0:T(1024)S(1)} %convert_element_type.196, pred[512]{0:T(512)(128)(4,1)S(1)} %copy-done.37, f32[512,3072]{1,0:T(8,128)} %fusion.60, f32[3072]{0:T(1024)S(1)} %copy-done.24), kind=kOutput, calls=%fused_computation.78 | convolution fusion | flops 2433220608 | bytes 13385216 | tf_op jit(solution)/shard_map/dot_general | solution.py:20
  422.8 6.6 fusion.49
  429.4 42.5 %all-reduce.27 = (bf16[768]{0:T(1024)(128)(2,1)S(1)}, bf16[768]{0:T(1024)(128)(2,1)S(1)}, bf16[768]{0:T(1024)(128)(2,1)S(1)}, bf16[3072]{0:T(1024)(128)(2,1)S(1)...) all-reduce(f32[768]{0:T(1024)S(1)} %slice.25, ...), channel_id=6, replica_groups=mesh['dp'=16,'seq'=2] {'dp','seq'}, use_global_device_ids=true, to_apply=%region_22.23.clone | all-reduce | flops 9216 | bytes 55296
  474.5 5.2 all-reduce.29
  488.4 4.6 all_gather.92
  493.7 12.8 %reduce-scatter.5.cloned.1.call-done = f32[24,2304]{1,0:T(8,128)} async-done(((f32[768,2304]{1,0:T(8,128)}), f32[24,2304]{1,0:T(8,128)}) %reduce-scatter.5.cloned.1.call-update) | async-done | bytes 221200 | tf_op jit(solution)/shard_map/reduce_scatter | solution.py:246
  507.5 5.4 all_gather.91
  513.7 133.5 %reduce-scatter.9.cloned.1.call-done = f32[24,3072]{1,0:T(8,128)} async-done(((f32[768,3072]{1,0:T(8,128)}), f32[24,3072]{1,0:T(8,128)}) %reduce-scatter.9.cloned.1.call-update) | async-done | bytes 294928 | tf_op jit(solution)/shard_map/reduce_scatter | solution.py:246
  648.2 5.8 all_gather.93
  654.9 134.0 %reduce-scatter.11.cloned.1.call-done = f32[96,768]{1,0:T(8,128)} async-done(((f32[3072,768]{1,0:T(8,128)}), f32[96,768]{1,0:T(8,128)}) %reduce-scatter.11.cloned.1.call-update) | async-done | bytes 294928 | tf_op jit(solution)/shard_map/reduce_scatter | solution.py:246
  789.9 5.8 all_gather.94
  (295 shorter events, 94.0 us)
Async XLA Ops:
  7.2 79.0 %all-gather.5.cloned.1.call-start = ((), (), s32[]{:S(2)}) async-start(), calls=%async_computation.8 | async-start | bytes 3760128 | tf_op jit(solution)/shard_map/all_gather | solution.py:88
  7.9 174.3 %all-gather.7.cloned.1.call-start = ((), (), s32[]{:S(2)}) async-start(), calls=%async_computation.9 | async-start | bytes 1253376 | tf_op jit(solution)/shard_map/all_gather | solution.py:89
  8.7 178.3 %all-gather.9.cloned.1.call-start = ((), (), s32[]{:S(2)}) async-start(), calls=%async_computation.10 | async-start | bytes 5013504 | tf_op jit(solution)/shard_map/all_gather | solution.py:90
  83.2 2.9 copy-start.30
  83.3 2.9 copy-start.17
  98.9 4.6 copy-start.41
  98.9 27.5 %all-to-all-start = ((bf16[512,3,2,384]{3,0,1,2:T(8,128)(2,1)}), bf16[512,3,2,384]{3,0,1,2:T(8,128)(2,1)S(1)}, u32[]{:S(2)}, u32[]{:S(2)}) async-start(bf16[512,3,2,384]{3,0,1,2:T(8,128)(2,1)} %copy.93), calls=%async_computation | async-start | bytes 4718592 | tf_op jit(solution)/shard_map/all_to_all | solution.py:117
  102.9 106.3 %all-gather.11.cloned.1.call-start = ((), (), s32[]{:S(2)}) async-start(), calls=%async_computation.11 | async-start | bytes 5013504 | tf_op jit(solution)/shard_map/all_gather | solution.py:91
  162.2 12.8 %all-to-all-start.1 = ((bf16[2,2,98304]{2,1,0:T(2,128)(2,1)}), bf16[2,2,98304]{2,1,0:T(2,128)(2,1)}, u32[]{:S(2)}, u32[]{:S(2)}) async-start(bf16[2,2,98304]{2,1,0:T(2,128)(2,1)} %reshape.425), calls=%async_computation.1 | async-start | bytes 1572864 | tf_op jit(solution)/shard_map/all_to_all | solution.py:151
  167.0 20.0 %copy-start.32 = (f32[768]{0:T(1024)}, f32[768]{0:T(1024)S(1)}, u32[]{:S(2)}) copy-start(f32[768]{0:T(1024)S(1)} %convert_element_type.192) | copy-start | bytes 9220
  167.0 55.4 %copy-start.19 = (f32[768]{0:T(1024)}, f32[768]{0:T(1024)S(1)}, u32[]{:S(2)}) copy-start(f32[768]{0:T(1024)S(1)} %convert_element_type.191) | copy-start | bytes 9220
  167.0 42.1 %copy-start.23 = (f32[3072]{0:T(1024)}, f32[3072]{0:T(1024)S(1)}, u32[]{:S(2)}) copy-start(f32[3072]{0:T(1024)S(1)} %convert_element_type.194) | copy-start | bytes 36868
  167.1 55.2 %copy-start.36 = (pred[512]{0:T(512)(128)(4,1)}, pred[512]{0:T(512)(128)(4,1)S(1)}, u32[]{:S(2)}) copy-start(pred[512]{0:T(512)(128)(4,1)S(1)} %dynamic-slice_compare_fusion) | copy-start | bytes 1540
  185.5 36.9 %copy-start.13 = (f32[512]{0:T(512)}, f32[512]{0:T(512)S(1)}, u32[]{:S(2)}) copy-start(f32[512]{0:T(512)S(1)} %broadcast_multiply_fusion.4) | copy-start | bytes 6148
  186.9 35.4 %copy-start.26 = (f32[512]{0:T(512)}, f32[512]{0:T(512)S(1)}, u32[]{:S(2)}) copy-start(f32[512]{0:T(512)S(1)} %add_rsqrt_fusion) | copy-start | bytes 6148
  209.1 9.7 %copy-start.8 = (f32[512,768]{1,0:T(8,128)S(1)}, f32[512,768]{1,0:T(8,128)}, u32[]{:S(2)}) copy-start(f32[512,768]{1,0:T(8,128)} %copy-done.7) | copy-start | bytes 4718596
  209.1 9.7 %copy-start.39 = (bf16[768,3072]{1,0:T(8,128)(2,1)S(1)}, bf16[768,3072]{1,0:T(8,128)(2,1)}, u32[]{:S(2)}) copy-start(bf16[768,3072]{1,0:T(8,128)(2,1)} %all-gather.9.cloned.1.call-done) | copy-start | bytes 14155780
  218.8 3.6 copy-start.43
  218.8 3.6 copy-start.9
  226.9 15.9 %all-to-all-start.2 = ((bf16[512,2,384]{2,0,1:T(8,128)(2,1)}), bf16[512,2,384]{2,0,1:T(8,128)(2,1)}, u32[]{:S(2)}, u32[]{:S(2)}) async-start(bf16[512,2,384]{2,0,1:T(8,128)(2,1)} %bitcast.119), calls=%async_computation.2 | async-start | bytes 1572864 | tf_op jit(solution)/shard_map/all_to_all | solution.py:187
  231.2 256.3 %reduce-scatter.7.cloned.1.call-start = ((), (), s32[]{:S(2)}) async-start(), calls=%async_computation.13 | async-start | bytes 2433024 | tf_op jit(solution)/shard_map/reduce_scatter | solution.py:246
  235.1 271.4 %reduce-scatter.5.cloned.1.call-start = ((), (), s32[]{:S(2)}) async-start(), calls=%async_computation.12 | async-start | bytes 7299072 | tf_op jit(solution)/shard_map/reduce_scatter | solution.py:246
  249.2 10.3 %copy-start.2 = (bf16[1024,6,64]{0,2,1:T(8,128)(2,1)}, bf16[1024,6,64]{0,2,1:T(8,128)(2,1)S(1)}, u32[]{:S(2)}) copy-start(bf16[1024,6,64]{0,2,1:T(8,128)(2,1)S(1)} %get-tuple-element.577) | copy-start | bytes 2359300 | tf_op jit(solution)/shard_map/while
  259.6 7.9 slice-start
  259.6 7.8 slice-start.1
  259.6 9.0 %slice-start.2 = ((s8[12582912]{0:T(1024)(128)(4,1)}), s8[4194304]{0:T(1024)(128)(4,1)S(1)}, s32[]{:S(2)}) async-start(s8[12582912]{0:T(1024)(128)(4,1)} %bitcast.106), calls=%async_computation.18 | async-start | bytes 8388608 | tf_op jit(solution)/shard_map/while
  273.6 7.0 copy-start
  273.6 13.0 %slice-start.3 = ((s8[6291456]{0:T(1024)(128)(4,1)}), s8[4194304]{0:T(1024)(128)(4,1)S(1)}, s32[]{:S(2)}) async-start(s8[6291456]{0:T(1024)(128)(4,1)} %bitcast.108), calls=%async_computation.19 | async-start | bytes 8388608 | tf_op jit(solution)/shard_map/while
  280.6 6.0 slice-start.4
  280.6 6.0 copy-start.10
  286.6 2.9 copy-start.3
  289.5 10.3 %copy-start.2 = (bf16[1024,6,64]{0,2,1:T(8,128)(2,1)}, bf16[1024,6,64]{0,2,1:T(8,128)(2,1)S(1)}, u32[]{:S(2)}) copy-start(bf16[1024,6,64]{0,2,1:T(8,128)(2,1)S(1)} %get-tuple-element.577) | copy-start | bytes 2359300 | tf_op jit(solution)/shard_map/while
  299.8 7.8 slice-start
  299.8 7.8 slice-start.1
  299.9 8.8 %slice-start.2 = ((s8[12582912]{0:T(1024)(128)(4,1)}), s8[4194304]{0:T(1024)(128)(4,1)S(1)}, s32[]{:S(2)}) async-start(s8[12582912]{0:T(1024)(128)(4,1)} %bitcast.106), calls=%async_computation.18 | async-start | bytes 8388608 | tf_op jit(solution)/shard_map/while
  313.7 7.5 copy-start
  313.7 14.0 %slice-start.3 = ((s8[6291456]{0:T(1024)(128)(4,1)}), s8[4194304]{0:T(1024)(128)(4,1)S(1)}, s32[]{:S(2)}) async-start(s8[6291456]{0:T(1024)(128)(4,1)} %bitcast.108), calls=%async_computation.19 | async-start | bytes 8388608 | tf_op jit(solution)/shard_map/while
  321.1 6.6 slice-start.4
  321.1 6.6 copy-start.10
  327.7 2.9 copy-start.3
  389.3 258.0 %reduce-scatter.9.cloned.1.call-start = ((), (), s32[]{:S(2)}) async-start(), calls=%async_computation.14 | async-start | bytes 9732096 | tf_op jit(solution)/shard_map/reduce_scatter | solution.py:246
  398.8 390.1 %reduce-scatter.11.cloned.1.call-start = ((), (), s32[]{:S(2)}) async-start(), calls=%async_computation.15 | async-start | bytes 9732096 | tf_op jit(solution)/shard_map/reduce_scatter | solution.py:246
  422.7 6.7 copy-start.21
  422.7 6.6 copy-start.22
  422.7 6.6 copy-start.25
  422.8 6.6 copy-start.34
  422.8 6.6 copy-start.35
  422.8 61.6 %copy-start.5 = (f32[512,768]{1,0:T(8,128)S(1)}, f32[512,768]{1,0:T(8,128)}, u32[]{:S(2)}) copy-start(f32[512,768]{1,0:T(8,128)} %copy-done.4) | copy-start | bytes 4718596
  (22 other events, 31.0 us)
Sparse Core Ops, SparseCore 0:
  10.3 50.7 all-gather.4
  63.4 36.7 all-gather.6
  102.5 52.3 all-gather.8
  157.1 51.9 all-gather.10
  237.0 98.1 reduce-scatter.6
  389.4 117.0 reduce-scatter.4
  512.4 134.7 reduce-scatter.8
  654.1 134.7 reduce-scatter.10
where the time goes:
time: 810 us; the launch traced here: 804 us
  waiting for transfers between devices  335 us (41%)
  blocking collectives  172 us (21%)
  matrix products  147 us (18%)
  local copies, waits for them, and re-layouts  65.1 us (8%)
  other arithmetic  45.9 us (6%)
  between operations  17.9 us (2%)
  starting transfers between devices  13.7 us (2%)
    reduce_scatter x4, waiting for transfers between devices, per_device(): lax.psum_scatter(stem_grads + branch_grads, ('dp', 'seq'), scatter_dimens...  280 us
    unnamed x3, blocking collectives  111 us
    all_to_all x1, blocking collectives, per_device(): lax.all_to_all(grad_side.reshape(group, 3, 1, local), 'seq', split_axis=0...  38.6 us
    dot_general x4, matrix products, dense_left(): lax.dot_general(left, right, (((0,), (0,)), ((), ())), preferred_element_...  30 us
    dot_general x4, matrix products, dense(): return jnp.dot(left, right, preferred_element_type=jnp.float32)  27.2 us
    unnamed x128, local copies, waits for them, and re-layouts  23.7 us
    all_to_all x1, waiting for transfers between devices, per_device(): lax.all_to_all(qkv.reshape(rows, 3, pair, local), 'seq', split_axis=2, co...  22.7 us
    all_gather x4, blocking collectives, per_device(): lax.all_gather(as_sent(halves), 'seq', axis=0, tiled=True)  21.7 us
  transfers between devices with their start and end apart: 11, of which 7 were waited for; matrix products, arithmetic and copies ran while one was open for 28% of the time, Pallas kernels for 0%

commit v1 on v0

--- a/solution.py
+++ b/solution.py
@@ -1,6 +1,8 @@
 import jax
 import jax.numpy as jnp
 from jax import lax
+from jax.experimental import pallas as pl
+from jax.experimental.pallas import tpu as pltpu
 from jax.sharding import PartitionSpec as P
 
 HEAD_DIM = 64
@@ -56,7 +58,7 @@
     )
 
 
-def per_device(
+def per_device_plain(
     tokens,
     lengths,
     w_qkv,
@@ -272,6 +274,979 @@
     )
 
 
+FAR = pl.DeviceIdType.MESH
+NT = (((1,), (1,)), ((), ()))
+BF = jnp.bfloat16
+F32 = jnp.float32
+
+
+def mul(left, right):
+    return jnp.dot(left, right, preferred_element_type=F32)
+
+
+def mul_nt(left, right):
+    return lax.dot_general(left, right, NT, preferred_element_type=F32)
+
+
+def flat(blocks):
+    return blocks.reshape(blocks.shape[0] * blocks.shape[1], blocks.shape[2])
+
+
+def normed(value):
+    width = value.shape[1]
+    mean = jnp.sum(value, axis=1, keepdims=True) * (1.0 / width)
+    centred = value - mean
+    spread = jnp.sum(centred * centred, axis=1, keepdims=True) * (1.0 / width)
+    inverse = lax.rsqrt(spread + EPSILON)
+    return (centred * inverse, inverse)
+
+
+def normed_back(grad, scaled, inverse, gain):
+    width = grad.shape[1]
+    shaped = grad * gain
+    inner = jnp.sum(shaped * scaled, axis=1, keepdims=True) * (1.0 / width)
+    outer = jnp.sum(shaped, axis=1, keepdims=True) * (1.0 / width)
+    return inverse * (shaped - outer - scaled * inner)
+
+
+def column_sum(value):
+    return jnp.sum(value, axis=0, keepdims=True)
+
+
+class Numbers:
+    def __init__(self):
+        self.used = 0
+
+    def take(self, count):
+        start = self.used
+        self.used = start + count
+        return start
+
+
+BIAS_Q, BIAS_V, BIAS_OUT, BIAS_DOWN, GAIN_1, SHIFT_1, GAIN_2, SHIFT_2, BIAS_UP = range(9)
+TABLE = 16
+FAR_COUNT = 160
+NEAR_COUNT = 32
+
+
+def fused_kernel(
+    lengths, table, tok, cot, own_q, own_o, own_u, own_d,
+    out, gtok, out_q, out_o, out_u, out_d, out_v,
+    wq, wo, wu, wd, gwq,
+    tok_far, first, first_t, qkv, k_t, v_t, lower, lse, o_t,
+    mixed_near, mixed, mixed_t, middle, second, second_t, gout, result,
+    hidden, hidden_t, gpre, gmix, gmix_head, gattn, dk, dv, dq_t, gqkv,
+    e_own, e_z, e_y, e_c, vec, gvec, v_z, v_y, v_c, v_x, v_sum,
+    r1_d, r2_d, r3_d, r5_d, r1_u, r2_u, r3_u, r5_u,
+    r1_o, r2_o, r3_o, r5_o, r1_q, r2_q, r3_q, r5_q,
+    gf_send, gf_recv,
+    near_sem, send_sem, recv_sem,
+):
+    d = lax.axis_index("dp")
+    s = lax.axis_index("seq")
+    z = lax.div(d, 4)
+    y = lax.rem(lax.div(d, 2), 2)
+    c = lax.rem(d, 2)
+    zs = wq.shape[0]
+    rows, width = tok.shape
+    group = 2 * rows
+    local = width // 2
+    pairs = local // 128
+    rq = width // (4 * zs)
+    rd = own_d.shape[0]
+    tile = 4 * rd
+    tiles = zs
+    z_peers = [(lax.rem(z + dz, zs) * 4 + y * 2 + c, s) for dz in range(1, zs)]
+    y_peer = (z * 4 + (1 - y) * 2 + c, s)
+    c_peer = (z * 4 + y * 2 + (1 - c), s)
+    x_peer = (d, 1 - s)
+    number = Numbers()
+    local_number = Numbers()
+
+    def far(src, dst, slot, device):
+        return pltpu.make_async_remote_copy(
+            src_ref=src, dst_ref=dst, send_sem=send_sem.at[slot], recv_sem=recv_sem.at[slot],
+            device_id=device, device_id_type=FAR,
+        )
+
+    def z_at(dz):
+        return lax.rem(z + zs - dz, zs)
+
+    def loop(count, body):
+        lax.fori_loop(0, count, lambda i, carry: (body(i), carry)[1], 0)
+
+    def block_rows(r, yy, cc):
+        return pl.ds(pl.multiple_of((yy * 2 + cc) * r, r), r)
+
+    barrier = pltpu.get_barrier_semaphore()
+    everyone = z_peers + [y_peer, c_peer, x_peer]
+    for peer in everyone:
+        pl.semaphore_signal(barrier, inc=1, device_id=peer, device_id_type=FAR)
+    pl.semaphore_wait(barrier, len(everyone))
+
+    class Gather:
+        def __init__(self, ref, r, columns, base):
+            self.ref, self.r, self.columns, self.base = ref, r, columns, base
+
+        def part(self, zz, yy, cc):
+            return self.ref.at[zz, block_rows(self.r, yy, cc), self.columns]
+
+        def layer(self, yy, cc):
+            return self.ref.at[:, block_rows(self.r, yy, cc), self.columns]
+
+        def z_copy(self, dz):
+            return far(self.part(z, y, c), self.part(z, y, c), self.base + dz - 1, z_peers[dz - 1])
+
+        def z_start(self):
+            for dz in range(1, zs):
+                self.z_copy(dz).start()
+
+        def z_wait(self):
+            for dz in range(1, zs):
+                block = self.part(z_at(dz), y, c)
+                far(block, block, self.base + dz - 1, z_peers[dz - 1]).wait_recv()
+
+        def y_copy(self, yy):
+            return far(self.layer(yy, c), self.layer(yy, c), self.base + zs - 1, y_peer)
+
+        def c_copy(self, yy, cc, other):
+            return far(self.layer(yy, cc), self.layer(yy, cc), self.base + zs + other, c_peer)
+
+        def relay(self):
+            self.z_wait()
+            self.y_copy(y).start()
+            self.c_copy(y, c, 0).start()
+
+        def relay_y(self):
+            self.y_copy(1 - y).wait_recv()
+            self.c_copy(1 - y, c, 1).start()
+
+        def finish(self):
+            self.c_copy(y, 1 - c, 0).wait_recv()
+            self.c_copy(1 - y, 1 - c, 1).wait_recv()
+
+        def sent(self):
+            for dz in range(1, zs):
+                self.z_copy(dz).wait_send()
+            self.y_copy(y).wait_send()
+            self.c_copy(y, c, 0).wait_send()
+            self.c_copy(1 - y, c, 1).wait_send()
+
+    steps = zs + 2
+    base_q = number.take(pairs * steps)
+
+    def gather_q(p):
+        return Gather(wq, rq, pl.ds(pl.multiple_of(p * local, 128), local), base_q + p * steps)
+
+    gather_o = Gather(wo, rq, pl.ds(0, width), number.take(steps))
+    halves_u = 2
+    span_u = wu.shape[2] // halves_u
+    gather_u = [Gather(wu, rq, pl.ds(i * span_u, span_u), number.take(steps)) for i in range(halves_u)]
+    gather_d = Gather(wd, rd, pl.ds(0, width), number.take(steps))
+
+    near_q = []
+    for p in range(pairs):
+        for part in range(3):
+            start = pl.multiple_of(part * width + s * local + p * 128, 128)
+            near_q.append(
+                pltpu.make_async_copy(
+                    own_q.at[:, pl.ds(start, 128)],
+                    wq.at[z, block_rows(rq, y, c), pl.ds(p * local + part * 128, 128)],
+                    near_sem.at[local_number.take(1)],
+                )
+            )
+    near_rest = []
+    for own, whole, r in ((own_o, wo, rq), (own_u, wu, rq), (own_d, wd, rd)):
+        near_rest.append(
+            pltpu.make_async_copy(
+                own, whole.at[z, block_rows(r, y, c), :], near_sem.at[local_number.take(1)]
+            )
+        )
+    for copy in near_q + near_rest:
+        copy.start()
+
+    base_e = number.take(zs + 1)
+    for dz in range(1, zs):
+        far(table, e_z.at[dz - 1], base_e + dz - 1, z_peers[dz - 1]).start()
+    send_tok = far(tok, tok_far, number.take(1), x_peer)
+    send_tok.start()
+    for copy in near_q:
+        copy.wait()
+    for p in range(pairs):
+        gather_q(p).z_start()
+
+    for dz in range(1, zs):
+        far(table, e_z.at[dz - 1], base_e + dz - 1, z_peers[dz - 1]).wait_recv()
+    total = table[...].astype(F32)
+    for dz in range(1, zs):
+        total = total + e_z[dz - 1].astype(F32)
+    e_own[0] = total.astype(BF)
+    y_table = far(e_own.at[0], e_y, base_e + zs - 1, y_peer)
+    y_table.start()
+
+    ends = []
+    end = jnp.int32(0)
+    for j in range(lengths.shape[1]):
+        end = end + lengths[0, j]
+        ends.append(end)
+    position = lax.broadcasted_iota(jnp.int32, (1, group), 1)
+    start = jnp.zeros((1, group), jnp.int32)
+    for end in ends[:-1]:
+        start = jnp.where(position >= end, end, start)
+    lower[...] = start
+    last_valid = ends[-2]
+
+    y_table.wait_recv()
+    total = total + e_y[...].astype(F32)
+    e_own[1] = total.astype(BF)
+    c_table = far(e_own.at[1], e_c, base_e + zs, c_peer)
+    c_table.start()
+    c_table.wait_recv()
+    total = total + e_c[...].astype(F32)
+    for i in range(TABLE):
+        vec[i] = total[i : i + 1, :]
+
+    def first_norm(source, at):
+        def body(i):
+            x = source[pl.ds(pl.multiple_of(i * 128, 128), 128), :].astype(F32)
+            scaled, unused = normed(x)
+            value = (scaled * vec[GAIN_1] + vec[SHIFT_1]).astype(BF)
+            there = pl.ds(pl.multiple_of(at + i * 128, 128), 128)
+            first[there, :] = value
+            first_t[:, there] = value.T
+
+        loop(rows // 128, body)
+
+    first_norm(tok, s * rows)
+
+    for p in range(pairs):
+        gather_q(p).relay()
+    for copy in near_rest:
+        copy.wait()
+    gather_o.z_start()
+    for part in gather_u:
+        part.z_start()
+
+    send_tok.wait_recv()
+    first_norm(tok_far, (1 - s) * rows)
+
+    base_mixed = number.take(pairs)
+    near_mixed = local_number.take(pairs)
+
+    def lanes(p, part):
+        return pl.ds(pl.multiple_of(p * local + part * 128, 128), 128)
+
+    def send_mixed(p):
+        there = pl.ds(pl.multiple_of(s * local + p * 128, 128), 128)
+        here = pl.ds(pl.multiple_of(p * 128, 128), 128)
+        away = pl.ds(pl.multiple_of((1 - s) * rows, 128), rows)
+        return far(mixed_near.at[away, here], mixed.at[:, there], base_mixed + p, x_peer)
+
+    def keep_mixed(p):
+        there = pl.ds(pl.multiple_of(s * local + p * 128, 128), 128)
+        here = pl.ds(pl.multiple_of(p * 128, 128), 128)
+        stay = pl.ds(pl.multiple_of(s * rows, 128), rows)
+        return pltpu.make_async_copy(
+            mixed_near.at[stay, here], mixed.at[:, there], near_sem.at[near_mixed + p]
+        )
+
+    side = 256
+    blocks = group // side
+    key_at = lax.broadcasted_iota(jnp.int32, (side, side), 0)
+    query_at = lax.broadcasted_iota(jnp.int32, (side, side), 1)
+    lane = lax.broadcasted_iota(jnp.int32, (side, 128), 1)
+
+    def head_lanes(value, h):
+        inside = (lane >= h * HEAD_DIM) & (lane < h * HEAD_DIM + HEAD_DIM)
+        return jnp.where(inside, value, 0.0).astype(BF)
+
+    def scores(p, keys_block, query, qi, j):
+        raw = mul_nt(keys_block, query)
+        ok = key_at + j * side >= lower[:, qi * side : (qi + 1) * side]
+        if j == qi:
+            ok = ok & (key_at <= query_at)
+        return jnp.where(ok, raw, MASKED)
+
+    scale = HEAD_DIM ** (-0.5)
+
+    def attend(p):
+        def head(h):
+            half = pl.ds(pl.multiple_of(h * HEAD_DIM, HEAD_DIM), HEAD_DIM)
+            for qi in range(blocks):
+                query = head_lanes(
+                    qkv[qi * side : (qi + 1) * side, lanes(p, 0)].astype(F32) * scale, h
+                )
+                raw = []
+                top = None
+                for j in range(qi + 1):
+                    block = scores(p, qkv[j * side : (j + 1) * side, lanes(p, 1)], query, qi, j)
+                    raw.append(block)
+                    high = jnp.max(block, axis=0, keepdims=True)
+                    top = high if top is None else jnp.maximum(top, high)
+                amount = jnp.zeros((1, side), F32)
+                gathered = jnp.zeros((HEAD_DIM, side), F32)
+                for j in range(qi + 1):
+                    weight = jnp.exp(raw[j] - top)
+                    amount = amount + column_sum(weight)
+                    gathered = gathered + mul(
+                        v_t[p, half, j * side : (j + 1) * side], weight.astype(BF)
+                    )
+                o_t[half, qi * side : (qi + 1) * side] = gathered / amount
+                lse[p, h, :, qi * side : (qi + 1) * side] = top + jnp.log(amount)
+
+        loop(2, head)
+        here = pl.ds(pl.multiple_of(p * 128, 128), 128)
+        for qi in range(blocks):
+            at = slice(qi * side, (qi + 1) * side)
+            mixed_near[at, here] = o_t[:, at].T.astype(BF)
+
+    def project(p):
+        zero = jnp.zeros((1, 128), F32)
+        there = pl.ds(pl.multiple_of(s * local + p * 128, 128), 128)
+        bias = jnp.concatenate([vec[BIAS_Q, :, there], zero, vec[BIAS_V, :, there]], axis=1)
+        weight = flat(wq[:, :, pl.ds(pl.multiple_of(p * local, 128), local)])
+
+        def body(i):
+            at = pl.ds(pl.multiple_of(i * side, side), side)
+            value = (mul(first[at, :], weight) + bias).astype(BF)
+            qkv[at, pl.ds(pl.multiple_of(p * local, 128), local)] = value
+            k_t[p, :, at] = value[:, 128:256].T
+            v_t[p, :, at] = value[:, 256:384].T
+
+        loop(blocks, body)
+
+    def pair_forward(p):
+        gather_q(p).relay_y()
+        gather_q(p).finish()
+        project(p)
+        attend(p)
+        send_mixed(p).start()
+        keep_mixed(p).start()
+
+        @pl.when(p == 0)
+        def _():
+            gather_o.relay()
+            gather_u[0].relay()
+
+        @pl.when(p == 1)
+        def _():
+            gather_u[1].relay()
+            gather_d.z_start()
+
+    loop(pairs, pair_forward)
+
+    gather_o.relay_y()
+    gather_u[0].relay_y()
+    gather_o.finish()
+    for p in range(pairs):
+        keep_mixed(p).wait()
+    for p in range(pairs):
+        far(
+            mixed_near.at[pl.ds(0, rows), pl.ds(0, 128)],
+            mixed.at[:, pl.ds(pl.multiple_of((1 - s) * local + p * 128, 128), 128)],
+            base_mixed + p, x_peer,
+        ).wait_recv()
+
+    def project_out(i):
+        at = pl.ds(pl.multiple_of(i * 128, 128), 128)
+        near = mixed[at, :]
+        mixed_t[:, at] = near.T
+        value = tok[at, :].astype(F32) + mul(near, flat(wo[...])) + vec[BIAS_OUT]
+        middle[at, :] = value
+        result[at, :] = value + vec[BIAS_DOWN]
+        scaled, unused = normed(value)
+        rounded = (scaled * vec[GAIN_2] + vec[SHIFT_2]).astype(BF)
+        second[at, :] = rounded
+        second_t[:, at] = rounded.T
+        spot = s * rows + i * 128 + lax.broadcasted_iota(jnp.int32, (128, width), 0)
+        gout[at, :] = jnp.where(spot < last_valid, cot[at, :].astype(F32), 0.0).astype(BF)
+        gtok[at, :] = jnp.zeros((128, width), F32)
+
+    loop(rows // 128, project_out)
+
+    gather_u[1].relay_y()
+    gather_d.relay()
+    gather_u[0].finish()
+    gather_u[1].finish()
+    gather_d.relay_y()
+    gather_d.finish()
+    for part in gather_u + [gather_d]:
+        part.sent()
+
+    base_sib = number.take(tiles * 4)
+    base_ys = number.take(tiles * 2)
+    base_zd = number.take(zs - 1)
+    base_zu = number.take(tiles * (zs - 1))
+    base_xs = number.take(2)
+
+    def tile_lanes(t):
+        return pl.ds(pl.multiple_of(t * tile, 128), tile)
+
+    def sib_d(t, yy):
+        return far(
+            wd.at[t, block_rows(rd, yy, 1 - c), :],
+            r1_d.at[t, pl.ds(pl.multiple_of(yy * rd, rd), rd), :],
+            base_sib + t * 4 + yy, c_peer,
+        )
+
+    def sib_u(t, yy):
+        return far(
+            wu.at[:, block_rows(rq, yy, 1 - c), tile_lanes(t)],
+            r1_u.at[:, pl.ds(pl.multiple_of(yy * rq, rq), rq), tile_lanes(t)],
+            base_sib + t * 4 + 2 + yy, c_peer,
+        )
+
+    def sib_start(t):
+        for yy in (1 - y, y):
+            sib_d(t, yy).start()
+            sib_u(t, yy).start()
+
+    def y_d(t):
+        return far(
+            r1_d.at[t, pl.ds(pl.multiple_of((1 - y) * rd, rd), rd), :], r2_d.at[t],
+            base_ys + t * 2, y_peer,
+        )
+
+    def y_u(t):
+        return far(
+            r1_u.at[:, pl.ds(pl.multiple_of((1 - y) * rq, rq), rq), tile_lanes(t)],
+            r2_u.at[:, :, tile_lanes(t)], base_ys + t * 2 + 1, y_peer,
+        )
+
+    def y_start(t):
+        yy = 1 - y
+        sib_d(t, yy).wait_recv()
+        at = pl.ds(pl.multiple_of(yy * rd, rd), rd)
+        r1_d[t, at, :] = (
+            r1_d[t, at, :].astype(F32) + wd[t, block_rows(rd, yy, c), :].astype(F32)
+        ).astype(BF)
+        sib_u(t, yy).wait_recv()
+        at = pl.ds(pl.multiple_of(yy * rq, rq), rq)
+        for zz in range(zs):
+            r1_u[zz, at, tile_lanes(t)] = (
+                r1_u[zz, at, tile_lanes(t)].astype(F32)
+                + wu[zz, block_rows(rq, yy, c), tile_lanes(t)].astype(F32)
+            ).astype(BF)
+        y_d(t).start()
+        y_u(t).start()
+
+    def z_d(t, dz):
+        return far(r2_d.at[t], r3_d.at[dz - 1], base_zd + dz - 1, (t * 4 + y * 2 + c, s))
+
+    def z_u(t, dz):
+        return far(
+            r2_u.at[lax.rem(z + dz, zs), :, tile_lanes(t)], r3_u.at[dz - 1, :, tile_lanes(t)],
+            base_zu + t * (zs - 1) + dz - 1, z_peers[dz - 1],
+        )
+
+    def z_start(t):
+        sib_d(t, y).wait_recv()
+        y_d(t).wait_recv()
+        at = pl.ds(pl.multiple_of(y * rd, rd), rd)
+        r2_d[t] = (
+            r2_d[t].astype(F32)
+            + r1_d[t, at, :].astype(F32)
+            + wd[t, block_rows(rd, y, c), :].astype(F32)
+        ).astype(BF)
+        sib_u(t, y).wait_recv()
+        y_u(t).wait_recv()
+        at = pl.ds(pl.multiple_of(y * rq, rq), rq)
+        for zz in range(zs):
+            r2_u[zz, :, tile_lanes(t)] = (
+                r2_u[zz, :, tile_lanes(t)].astype(F32)
+                + r1_u[zz, at, tile_lanes(t)].astype(F32)
+                + wu[zz, block_rows(rq, y, c), tile_lanes(t)].astype(F32)
+            ).astype(BF)
+        dz = lax.rem(t + zs - z, zs)
+
+        @pl.when(dz > 0)
+        def _():
+            z_d(t, dz).start()
+
+        for step in range(1, zs):
+            z_u(t, step).start()
+
+    sub = 256
+
+    def feed(t):
+        def part(u):
+            at = pl.ds(pl.multiple_of(t * tile + u * sub, 128), sub)
+            near = pl.ds(pl.multiple_of(u * sub, sub), sub)
+            pre = mul(second[...], flat(wu[:, :, at])) + vec[BIAS_UP + t, :, near]
+            bent = jnp.tanh(SLOPE * (pre + CUBIC * pre * pre * pre))
+            value = (0.5 * pre * (1.0 + bent)).astype(BF)
+            slope = 0.5 * (1.0 + bent) + 0.5 * pre * (1.0 - bent * bent) * SLOPE * (
+                1.0 + 3.0 * CUBIC * pre * pre
+            )
+            hidden[:, near] = value
+            hidden_t[near, :] = value.T
+            grad = (mul_nt(gout[...], wd[t, near, :]) * slope).astype(BF)
+            gpre[:, near] = grad
+            gvec[BIAS_UP + t, :, near] = column_sum(grad.astype(F32))
+
+        loop(tile // sub, part)
+
+        def add(i):
+            at = pl.ds(pl.multiple_of(i * side, side), side)
+            result[at, :] += mul(hidden[at, :], wd[t])
+            gtok[at, :] += mul_nt(gpre[at, :], flat(wu[:, :, tile_lanes(t)]))
+
+        loop(rows // side, add)
+
+        def weigh(m):
+            at = pl.ds(pl.multiple_of(m * rd, rd), rd)
+            wd[t, at, :] = mul(hidden_t[at, :], gout[...]).astype(BF)
+
+        loop(4, weigh)
+
+        def weigh_up(m):
+            at = pl.ds(pl.multiple_of(m * 4 * rq, 4 * rq), 4 * rq)
+            wu[m, :, tile_lanes(t)] = mul(second_t[at, :], gpre[...]).astype(BF)
+
+        loop(zs, weigh_up)
+        sib_start(t)
+
+        @pl.when(t > 0)
+        def _():
+            y_start(t - 1)
+
+    loop(tiles, feed)
+
+    for row in (BIAS_Q, BIAS_V, BIAS_OUT, BIAS_DOWN, GAIN_1, SHIFT_1, GAIN_2, SHIFT_2):
+        gvec[row] = jnp.zeros((1, width), F32)
+    for row in range(BIAS_UP + tiles, TABLE):
+        gvec[row] = jnp.zeros((1, width), F32)
+
+    def middle_back(i):
+        at = pl.ds(pl.multiple_of(i * 128, 128), 128)
+        scaled, inverse = normed(middle[at, :])
+        grad = gtok[at, :]
+        ahead = gout[at, :].astype(F32)
+        gvec[GAIN_2] += column_sum(grad * scaled)
+        gvec[SHIFT_2] += column_sum(grad)
+        gvec[BIAS_DOWN] += column_sum(ahead)
+        total = ahead + normed_back(grad, scaled, inverse, vec[GAIN_2])
+        middle[at, :] = total
+        rounded = total.astype(BF)
+        gattn[at, :] = rounded
+        gvec[BIAS_OUT] += column_sum(rounded.astype(F32))
+        gmix[at, :] = mul_nt(rounded, flat(wo[...])).astype(BF)
+        spot = s * rows + i * 128 + lax.broadcasted_iota(jnp.int32, (128, width), 0)
+        out[at, :] = jnp.where(spot < last_valid, result[at, :], 0.0).astype(BF)
+
+    loop(rows // 128, middle_back)
+
+    slot_gmix = number.take(1)
+    send_gmix = far(
+        gmix.at[:, pl.ds(pl.multiple_of((1 - s) * local, 128), local)],
+        gmix_head.at[pl.ds(pl.multiple_of(s * rows, 128), rows), :],
+        slot_gmix, x_peer,
+    )
+    keep_gmix = pltpu.make_async_copy(
+        gmix.at[:, pl.ds(pl.multiple_of(s * local, 128), local)],
+        gmix_head.at[pl.ds(pl.multiple_of(s * rows, 128), rows), :],
+        near_sem.at[local_number.take(1)],
+    )
+    send_gmix.start()
+    keep_gmix.start()
+    y_start(tiles - 1)
+
+    gather_o.sent()
+
+    def weigh_out(m):
+        at = pl.ds(pl.multiple_of(m * 4 * rq, 4 * rq), 4 * rq)
+        wo[m] = mul(mixed_t[at, :], gattn[...]).astype(BF)
+
+    loop(zs, weigh_out)
+
+    class Spread:
+        def __init__(self, ref, columns, r1, r2, r3, base):
+            self.ref, self.columns, self.r1, self.r2, self.r3 = ref, columns, r1, r2, r3
+            self.base = base
+
+        def sib(self, yy):
+            return far(
+                self.ref.at[:, block_rows(rq, yy, 1 - c), self.columns],
+                self.r1.at[:, pl.ds(pl.multiple_of(yy * rq, rq), rq), self.columns],
+                self.base + yy, c_peer,
+            )
+
+        def sib_start(self):
+            self.sib(1 - y).start()
+            self.sib(y).start()
+
+        def along_y(self):
+            return far(
+                self.r1.at[:, pl.ds(pl.multiple_of((1 - y) * rq, rq), rq), self.columns],
+                self.r2.at[:, :, self.columns], self.base + 2, y_peer,
+            )
+
+        def y_start(self):
+            self.sib(1 - y).wait_recv()
+            at = pl.ds(pl.multiple_of((1 - y) * rq, rq), rq)
+            for zz in range(zs):
+                self.r1[zz, at, self.columns] = (
+                    self.r1[zz, at, self.columns].astype(F32)
+                    + self.ref[zz, block_rows(rq, 1 - y, c), self.columns].astype(F32)
+                ).astype(BF)
+            self.along_y().start()
+
+        def along_z(self, dz):
+            return far(
+                self.r2.at[lax.rem(z + dz, zs), :, self.columns],
+                self.r3.at[dz - 1, :, self.columns], self.base + 2 + dz, z_peers[dz - 1],
+            )
+
+        def z_start(self):
+            self.sib(y).wait_recv()
+            self.along_y().wait_recv()
+            at = pl.ds(pl.multiple_of(y * rq, rq), rq)
+            for zz in range(zs):
+                self.r2[zz, :, self.columns] = (
+                    self.r2[zz, :, self.columns].astype(F32)
+                    + self.r1[zz, at, self.columns].astype(F32)
+                    + self.ref[zz, block_rows(rq, y, c), self.columns].astype(F32)
+                ).astype(BF)
+            for dz in range(1, zs):
+                self.along_z(dz).start()
+
+        def z_finish(self):
+            total = self.r2[z, :, self.columns].astype(F32)
+            for dz in range(1, zs):
+                self.along_z(dz).wait_recv()
+                total = total + self.r3[dz - 1, :, self.columns].astype(F32)
+            return total
+
+        def sent(self):
+            self.sib(0).wait_send()
+            self.sib(1).wait_send()
+            self.along_y().wait_send()
+            for dz in range(1, zs):
+                self.along_z(dz).wait_send()
+
+    spread_steps = zs + 2
+    sum_o = Spread(wo, pl.ds(0, width), r1_o, r2_o, r3_o, number.take(spread_steps))
+    base_sq = number.take(pairs * spread_steps)
+
+    def sum_q(p):
+        return Spread(
+            gwq, pl.ds(pl.multiple_of(p * local, 128), local), r1_q, r2_q, r3_q,
+            base_sq + p * spread_steps,
+        )
+
+    sum_o.sib_start()
+    send_gmix.wait_send()
+    keep_gmix.wait()
+    far(
+        gmix.at[:, pl.ds(0, local)],
+        gmix_head.at[pl.ds(pl.multiple_of((1 - s) * rows, 128), rows), :],
+        slot_gmix, x_peer,
+    ).wait_recv()
+    sum_o.y_start()
+
+    def attend_back(p):
+        dk[...] = jnp.zeros_like(dk)
+        dv[...] = jnp.zeros_like(dv)
+
+        def head(h):
+            half = pl.ds(pl.multiple_of(h * HEAD_DIM, HEAD_DIM), HEAD_DIM)
+            here = pl.ds(pl.multiple_of(p * 128, 128), 128)
+            for qi in range(blocks):
+                at = slice(qi * side, (qi + 1) * side)
+                query = head_lanes(qkv[at, lanes(p, 0)].astype(F32) * scale, h)
+                grad = head_lanes(gmix_head[at, here].astype(F32), h)
+                level = lse[p, h, :, at]
+                weights, slopes = [], []
+                centre = jnp.zeros((1, side), F32)
+                for j in range(qi + 1):
+                    there = slice(j * side, (j + 1) * side)
+                    raw = scores(p, qkv[there, lanes(p, 1)], query, qi, j)
+                    weight = jnp.exp(raw - level)
+                    slope = mul_nt(qkv[there, lanes(p, 2)], grad)
+                    centre = centre + column_sum(weight * slope)
+                    weights.append(weight)
+                    slopes.append(slope)
+                total = jnp.zeros((HEAD_DIM, side), F32)
+                for j in range(qi + 1):
+                    there = slice(j * side, (j + 1) * side)
+                    bend = (weights[j] * (slopes[j] - centre)).astype(BF)
+                    dk[there, :] += mul(bend, query)
+                    dv[there, :] += mul(weights[j].astype(BF), grad)
+                    total = total + mul(k_t[p, half, there], bend)
+                dq_t[half, at] = total * scale
+
+        loop(2, head)
+        for qi in range(blocks):
+            at = slice(qi * side, (qi + 1) * side)
+            gqkv[at, lanes(p, 0)] = dq_t[:, at].T.astype(BF)
+            gqkv[at, lanes(p, 1)] = dk[at, :].astype(BF)
+            gqkv[at, lanes(p, 2)] = dv[at, :].astype(BF)
+        own = pl.ds(pl.multiple_of(s * local + p * 128, 128), 128)
+        gvec[BIAS_Q, :, own] = column_sum(gqkv[:, lanes(p, 0)].astype(F32))
+        gvec[BIAS_V, :, own] = column_sum(gqkv[:, lanes(p, 2)].astype(F32))
+        both = pl.ds(pl.multiple_of(p * local, 128), local)
+
+        def weigh(m):
+            at = pl.ds(pl.multiple_of(m * 4 * rq, 4 * rq), 4 * rq)
+            gwq[m, :, both] = mul(first_t[at, :], gqkv[:, both]).astype(BF)
+
+        loop(zs, weigh)
+
+    def pair_back(p):
+        z_start(p)
+        attend_back(p)
+        sum_q(p).sib_start()
+
+        @pl.when(p > 0)
+        def _():
+            sum_q(p - 1).y_start()
+
+    loop(pairs, pair_back)
+
+    base_gf = number.take(rows // side)
+
+    def send_gf(i):
+        at = pl.ds(pl.multiple_of(i * side, side), side)
+        return far(gf_send.at[at, :], gf_recv.at[at, :], base_gf + i, x_peer)
+
+    def first_back(i, source, at):
+        there = pl.ds(pl.multiple_of(at + i * side, side), side)
+        grad = mul_nt(gqkv[there, :], flat(wq[...]))
+        scaled, unused = normed(source[pl.ds(pl.multiple_of(i * side, side), side), :].astype(F32))
+        gvec[GAIN_1] += column_sum(grad * scaled)
+        gvec[SHIFT_1] += column_sum(grad)
+        return grad
+
+    def away(i):
+        grad = first_back(i, tok_far, (1 - s) * rows)
+        gf_send[pl.ds(pl.multiple_of(i * side, side), side), :] = grad.astype(BF)
+        send_gf(i).start()
+
+    loop(rows // side, away)
+    sum_q(pairs - 1).y_start()
+
+    def stay(i):
+        gtok[pl.ds(pl.multiple_of(i * side, side), side), :] = first_back(i, tok, s * rows)
+
+    loop(rows // side, stay)
+
+    base_v = number.take(zs + 2)
+    for dz in range(1, zs):
+        far(gvec, v_z.at[dz - 1], base_v + dz - 1, z_peers[dz - 1]).start()
+    z_start(tiles - 1)
+    sum_o.z_start()
+    for dz in range(1, zs):
+        far(gvec, v_z.at[dz - 1], base_v + dz - 1, z_peers[dz - 1]).wait_recv()
+    for i in range(TABLE):
+        total = gvec[i]
+        for dz in range(1, zs):
+            total = total + v_z[dz - 1, i]
+        v_sum[0, i] = total
+    vy = far(v_sum.at[0], v_y, base_v + zs - 1, y_peer)
+    vy.start()
+    for p in range(pairs):
+        sum_q(p).z_start()
+    vy.wait_recv()
+    v_sum[1] = v_sum[0] + v_y[...]
+    vc = far(v_sum.at[1], v_c, base_v + zs, c_peer)
+    vc.start()
+    vc.wait_recv()
+    v_sum[2] = v_sum[1] + v_c[...]
+    vx = far(v_sum.at[2], v_x, base_v + zs + 1, x_peer)
+    vx.start()
+
+    total = r2_d[z].astype(F32)
+    for dz in range(1, zs):
+        far(r2_d.at[0], r3_d.at[dz - 1], base_zd + dz - 1, z_peers[dz - 1]).wait_recv()
+        total = total + r3_d[dz - 1].astype(F32)
+    r5_d[0] = total.astype(BF)
+    xd = far(r5_d.at[0], r5_d.at[1], base_xs, x_peer)
+    xd.start()
+    for t in range(tiles):
+        for dz in range(1, zs):
+            z_u(t, dz).wait_recv()
+
+    def finish_u(t):
+        total = r2_u[z, :, tile_lanes(t)].astype(F32)
+        for dz in range(1, zs):
+            total = total + r3_u[dz - 1, :, tile_lanes(t)].astype(F32)
+        r5_u[0, :, tile_lanes(t)] = total.astype(BF)
+
+    loop(tiles, finish_u)
+    xu = far(r5_u.at[0], r5_u.at[1], base_xs + 1, x_peer)
+    xu.start()
+    r5_o[0] = sum_o.z_finish().astype(BF)
+    xo = far(r5_o.at[0], r5_o.at[1], number.take(1), x_peer)
+    xo.start()
+    for p in range(pairs):
+        r5_q[s, :, p * local : (p + 1) * local] = sum_q(p).z_finish().astype(BF)
+    slot_q = number.take(1)
+    xq = far(r5_q.at[s], r5_q.at[s], slot_q, x_peer)
+    xq.start()
+
+    for i in range(rows // side):
+        send_gf(i).wait_recv()
+
+    def last(i):
+        at = pl.ds(pl.multiple_of(i * 128, 128), 128)
+        scaled, inverse = normed(tok[at, :].astype(F32))
+        grad = gtok[at, :] + gf_recv[at, :].astype(F32)
+        gtok[at, :] = middle[at, :] + normed_back(grad, scaled, inverse, vec[GAIN_1])
+
+    loop(rows // 128, last)
+
+    vx.wait_recv()
+    out_v[...] = v_sum[2] + v_x[...]
+    xd.wait_recv()
+    out_d[...] = r5_d[0].astype(F32) + r5_d[1].astype(F32)
+    xu.wait_recv()
+
+    def store_u(t):
+        out_u[:, tile_lanes(t)] = r5_u[0, :, tile_lanes(t)].astype(F32) + r5_u[1, :, tile_lanes(t)].astype(F32)
+
+    loop(tiles, store_u)
+    xo.wait_recv()
+    out_o[...] = r5_o[0].astype(F32) + r5_o[1].astype(F32)
+    far(r5_q.at[1 - s], r5_q.at[1 - s], slot_q, x_peer).wait_recv()
+    for half in range(2):
+        for p in range(pairs):
+            for part in range(3):
+                at = part * width + half * local + p * 128
+                out_q[:, at : at + 128] = r5_q[
+                    half, :, p * local + part * 128 : p * local + part * 128 + 128
+                ].astype(F32)
+
+    for dz in range(1, zs):
+        far(table, e_z.at[dz - 1], base_e + dz - 1, z_peers[dz - 1]).wait_send()
+        far(gvec, v_z.at[dz - 1], base_v + dz - 1, z_peers[dz - 1]).wait_send()
+        far(r2_d.at[0], r3_d.at[dz - 1], base_zd + dz - 1, z_peers[dz - 1]).wait_send()
+    for copy in (y_table, c_table, send_tok, vy, vc, vx, xd, xu, xo, xq):
+        copy.wait_send()
+    for p in range(pairs):
+        gather_q(p).sent()
+        send_mixed(p).wait_send()
+        sum_q(p).sent()
+    sum_o.sent()
+    for t in range(tiles):
+        for yy in range(2):
+            sib_d(t, yy).wait_send()
+            sib_u(t, yy).wait_send()
+        y_d(t).wait_send()
+        y_u(t).wait_send()
+        for dz in range(1, zs):
+            z_u(t, dz).wait_send()
+    for i in range(rows // side):
+        send_gf(i).wait_send()
+
+
+def fused_fits(tokens, lengths, own_q, own_d, shards, pair):
+    rows, width = tokens.shape
+    return (
+        shards == 16
+        and pair == 2
+        and rows % 256 == 0
+        and (width // pair) % 128 == 0
+        and own_q.shape[0] % 16 == 0
+        and own_d.shape[0] % 64 == 0
+        and own_d.shape[0] * shards == 4 * width
+    )
+
+
+def fused(tokens, lengths, w_qkv, w_out, w_up, w_down, small, bias_up, cotangent):
+    rows, width = tokens.shape
+    shards = lax.axis_size("dp")
+    zs = shards // 4
+    d = lax.axis_index("dp")
+    rq, rd = w_qkv.shape[0], w_down.shape[0]
+    deep = 4 * rd * zs
+    group = 2 * rows
+    local = width // 2
+    pairs = local // 128
+    lane = jnp.arange(width)
+    own = jnp.where(lane // rq == d, jnp.tile(jnp.stack(small), (1, shards)), 0)
+    at = jnp.arange(zs)[:, None] * width + lane[None, :]
+    up = jnp.where(at // rd == d, jnp.tile(bias_up, (width // rd,))[None, :], 0)
+    table = jnp.concatenate([own, up, jnp.zeros((TABLE - 8 - zs, width), own.dtype)], axis=0)
+
+    def vm(shape, kind=BF):
+        return pltpu.VMEM(shape, kind)
+
+    scratch = [
+        vm((zs, 4 * rq, 3 * local)), vm((zs, 4 * rq, width)), vm((zs, 4 * rq, deep)),
+        vm((zs, 4 * rd, width)), vm((zs, 4 * rq, 3 * local)),
+        vm((rows, width)), vm((group, width)), vm((width, group)), vm((group, 3 * local)),
+        vm((pairs, 128, group)), vm((pairs, 128, group)), vm((1, group), jnp.int32),
+        vm((pairs, 2, 1, group), F32), vm((128, group), F32),
+        vm((group, local)), vm((rows, width)), vm((width, rows)), vm((rows, width), F32),
+        vm((rows, width)), vm((width, rows)), vm((rows, width)), vm((rows, width), F32),
+        vm((rows, 4 * rd)), vm((4 * rd, rows)), vm((rows, 4 * rd)), vm((rows, width)),
+        vm((group, local)), vm((rows, width)), vm((group, 128), F32), vm((group, 128), F32),
+        vm((128, group), F32), vm((group, 3 * local)),
+        vm((2, TABLE, width)), vm((zs - 1, TABLE, width)), vm((TABLE, width)), vm((TABLE, width)),
+        vm((TABLE, 1, width), F32), vm((TABLE, 1, width), F32), vm((zs - 1, TABLE, 1, width), F32),
+        vm((TABLE, 1, width), F32), vm((TABLE, 1, width), F32), vm((TABLE, 1, width), F32),
+        vm((3, TABLE, 1, width), F32),
+        vm((zs, 2 * rd, width)), vm((zs, rd, width)), vm((zs - 1, rd, width)), vm((2, rd, width)),
+        vm((zs, 2 * rq, deep)), vm((zs, rq, deep)), vm((zs - 1, rq, deep)), vm((2, rq, deep)),
+        vm((zs, 2 * rq, width)), vm((zs, rq, width)), vm((zs - 1, rq, width)), vm((2, rq, width)),
+        vm((zs, 2 * rq, 3 * local)), vm((zs, rq, 3 * local)), vm((zs - 1, rq, 3 * local)),
+        vm((2, rq, 3 * local)),
+        vm((rows, width)), vm((rows, width)),
+        pltpu.SemaphoreType.DMA((NEAR_COUNT,)),
+        pltpu.SemaphoreType.DMA((FAR_COUNT,)),
+        pltpu.SemaphoreType.DMA((FAR_COUNT,)),
+    ]
+    here = pl.BlockSpec(memory_space=pltpu.VMEM)
+    away = pl.BlockSpec(memory_space=pl.ANY)
+    return pl.pallas_call(
+        fused_kernel,
+        out_shape=(
+            jax.ShapeDtypeStruct((rows, width), BF),
+            jax.ShapeDtypeStruct((rows, width), F32),
+            jax.ShapeDtypeStruct((rq, 3 * width), F32),
+            jax.ShapeDtypeStruct((rq, width), F32),
+            jax.ShapeDtypeStruct((rq, deep), F32),
+            jax.ShapeDtypeStruct((rd, width), F32),
+            jax.ShapeDtypeStruct((TABLE, 1, width), F32),
+        ),
+        in_specs=[pl.BlockSpec(memory_space=pltpu.SMEM), here, here, here, away, away, away, away],
+        out_specs=[here] * 7,
+        scratch_shapes=scratch,
+        compiler_params=pltpu.CompilerParams(
+            collective_id=0, has_side_effects=True, vmem_limit_bytes=67_043_328
+        ),
+        name="block",
+    )(lengths, table, tokens, cotangent, w_qkv, w_out, w_up, w_down)
+
+
+def per_device(
+    tokens, lengths, w_qkv, w_out, w_up, w_down, bias_q, bias_v, bias_out, bias_up, bias_down,
+    gain_one, shift_one, gain_two, shift_two, cotangent,
+):
+    if not fused_fits(
+        tokens, lengths, w_qkv, w_down, lax.axis_size("dp"), lax.axis_size("seq")
+    ):
+        return per_device_plain(
+            tokens, lengths, w_qkv, w_out, w_up, w_down, bias_q, bias_v, bias_out, bias_up,
+            bias_down, gain_one, shift_one, gain_two, shift_two, cotangent,
+        )
+    small = [bias_q, bias_v, bias_out, bias_down, gain_one, shift_one, gain_two, shift_two]
+    out, gtok, gq, go, gu, gd, table = fused(
+        tokens, lengths, w_qkv, w_out, w_up, w_down, small, bias_up, cotangent
+    )
+    d = lax.axis_index("dp")
+    width = tokens.shape[1]
+    rq, rd = w_qkv.shape[0], w_down.shape[0]
+    own = lax.dynamic_slice_in_dim(table[:8, 0], d * rq, rq, axis=1)
+    up = lax.dynamic_slice_in_dim(
+        table[8:].reshape((TABLE - 8) * width), d * rd, rd, axis=0
+    )
+    return (
+        out, gtok, gq, go, gu, gd,
+        own[0], own[1], own[2], up, own[3], own[4], own[5], own[6], own[7],
+    )
+
+
 def solution(mesh):
     return jax.shard_map(
         per_device,

time: 810 us -> 246 us (0.30)
  waiting for transfers between devices: 335 us -> 0 us
  Pallas kernels: 0 us -> 233 us
  blocking collectives: 172 us -> 0 us
  matrix products: 147 us -> 0 us
  local copies, waits for them, and re-layouts: 65.1 us -> 10.2 us
  other arithmetic: 45.9 us -> 0.75 us
  between operations: 17.9 us -> 0.71 us
  starting transfers between devices: 13.7 us -> 0 us
    reduce_scatter x4 -> x0, waiting for transfers between devices: 280 us -> none  [per_device(): lax.psum_scatter(stem_grads + branch_grads, ('dp', 'seq'), scatter_dimens...]
    pallas_call x0 -> x1, Pallas kernels: none -> 233 us  [fused(): pl.pallas_call(fused_kernel, out_shape=(jax.ShapeDtypeStruct((rows, width...]
    dot_general x26 -> x0, matrix products: 147 us -> none  [the longest x4 30 us: dense_left(): lax.dot_general(left, right, (((0,), (0,)), ((), ())), preferred_element_...]
    unnamed x3 -> x0, blocking collectives: 111 us -> none
    all_to_all x1 -> x0, blocking collectives: 38.6 us -> none  [per_device(): lax.all_to_all(grad_side.reshape(group, 3, 1, local), 'seq', split_axis=0...]
    all_to_all x3 -> x0, waiting for transfers between devices: 38.2 us -> none  [the longest x1 22.7 us: per_device(): lax.all_to_all(qkv.reshape(rows, 3, pair, local), 'seq', split_axis=2, co...]
    convert_element_type x28 -> x0, other arithmetic: 21.7 us -> none  [the longest x2 10 us: attend_back(): grad_scores = (probs * (grad_probs - centre)).astype(jnp.bfloat16)]
    all_gather x4 -> x0, blocking collectives: 21.7 us -> none  [per_device(): lax.all_gather(as_sent(halves), 'seq', axis=0, tiled=True)]
  transfers between devices with their start and end apart: 11 -> 0, of which waited for: 7 -> 0; matrix products, arithmetic and copies ran while one was open for 28% -> 0% of each run, Pallas kernels for 0% -> 0%
where the time goes in v1:
time: 246 us; the launch traced here: 244 us
  Pallas kernels  233 us (95%)
  local copies, waits for them, and re-layouts  10.2 us (4%)
    pallas_call x1, Pallas kernels, fused(): pl.pallas_call(fused_kernel, out_shape=(jax.ShapeDtypeStruct((rows, width...  233 us
    unnamed x16, local copies, waits for them, and re-layouts  6.4 us

profile of v1, /device:TPU:0, one launch (start us, length us, event | category | flops | bytes accessed | tf_op | source)
XLA Modules:
  0.0 244.4 jit_solution(6207191934409283941)
XLA Ops:
  0.7 0.8 stack.35
  1.5 0.7 tile.8
  2.1 0.1 broadcast_in_dim.27
  2.2 0.1 fusion.2
  2.3 0.1 tile.7
  2.5 0.6 pad_maximum_fusion.table
  3.1 232.8 %block.1 = (bf16[512,768]{1,0:T(8,128)(2,1)}, f32[512,768]{1,0:T(8,128)}, f32[48,2304]{1,0:T(8,128)}, f32[48,768]{1,0:T(8,128)}, f32[48,3072]{1,0:T(8,128)}, /*index=5*/f32[192,768]{1,0:T(8,128)}, f32[16,1,768]{2,1,0:T(1,128)}) custom-call(s32[1,6]{1,0:T(1,128)} %lengths.1, bf16[16,768]{1,0:T(8,128)(2,1)} %pad_maximum_fusion.table, bf16[512,768]{1,0:T(8,128)(2,1)} %tok.1, ...), custom_call_target="tpu_custom_call" | custom-call | tf_op jit(solution)/shard_map/block/pallas_call | solution.py:1201
  235.9 0.0 copy-start
  235.9 0.9 fusion.15
  236.8 0.6 dynamic_slice.7
  237.4 0.6 fusion.7
  238.0 2.1 copy.37
  240.1 0.0 copy-done
  240.1 0.0 copy-start.3
  240.1 0.0 copy-start.4
  240.1 0.0 copy-start.2
  240.1 1.1 copy.38
  241.2 0.1 copy-done.3
  241.4 0.0 copy-start.1
  241.4 0.8 copy.39
  242.1 0.0 copy-done.4
  242.1 0.7 copy.40
  242.8 0.0 copy-done.2
  242.8 0.8 copy.41
  243.6 0.0 copy-done.1
  243.6 0.8 copy.42
  (5 shorter events, 0.0 us)
Async XLA Ops:
  235.9 4.2 %copy-start = (f32[512,768]{1,0:T(8,128)S(1)}, f32[512,768]{1,0:T(8,128)}, u32[]{:S(2)}) copy-start(f32[512,768]{1,0:T(8,128)} %get-tuple-element.55) | copy-start | bytes 4718596
  240.1 1.3 copy-start.3
  240.1 2.0 copy-start.4
  240.1 2.7 %copy-start.2 = (f32[48,3072]{1,0:T(8,128)S(1)}, f32[48,3072]{1,0:T(8,128)}, u32[]{:S(2)}) copy-start(f32[48,3072]{1,0:T(8,128)} %get-tuple-element.58) | copy-start | bytes 1769476
  241.4 2.2 copy-start.1

commit v2 on v1

--- a/solution.py
+++ b/solution.py
@@ -325,21 +325,20 @@
 
 BIAS_Q, BIAS_V, BIAS_OUT, BIAS_DOWN, GAIN_1, SHIFT_1, GAIN_2, SHIFT_2, BIAS_UP = range(9)
 TABLE = 16
-FAR_COUNT = 160
+FAR_COUNT = 240
 NEAR_COUNT = 32
 
 
 def fused_kernel(
-    lengths, table, tok, cot, own_q, own_o, own_u, own_d,
+    lengths, table, tok_own, cot, own_q, own_o, own_u, own_d,
     out, gtok, out_q, out_o, out_u, out_d, out_v,
-    wq, wo, wu, wd, gwq,
-    tok_far, first, first_t, qkv, k_t, v_t, lower, lse, o_t,
-    mixed_near, mixed, mixed_t, middle, second, second_t, gout, result,
-    hidden, hidden_t, gpre, gmix, gmix_head, gattn, dk, dv, dq_t, gqkv,
+    wq, wo, wu, wd, gwq, gwd,
+    tok, tok_far, first, first_t, qkv, k_t, v_t, lower, lse, o_t,
+    mixed_near, mixed, mixed_t, middle, second, second_t, gout,
+    hidden, hidden_t, slope, gmix_head, dk, dv,
     e_own, e_z, e_y, e_c, vec, gvec, v_z, v_y, v_c, v_x, v_sum,
-    r1_d, r2_d, r3_d, r5_d, r1_u, r2_u, r3_u, r5_u,
+    r1_d, rx_d, ry_d, rz_d, r5_d, r1_u, r2_u, r3_u, r5_u,
     r1_o, r2_o, r3_o, r5_o, r1_q, r2_q, r3_q, r5_q,
-    gf_send, gf_recv,
     near_sem, send_sem, recv_sem,
 ):
     d = lax.axis_index("dp")
@@ -348,7 +347,7 @@
     y = lax.rem(lax.div(d, 2), 2)
     c = lax.rem(d, 2)
     zs = wq.shape[0]
-    rows, width = tok.shape
+    rows, width = tok_own.shape
     group = 2 * rows
     local = width // 2
     pairs = local // 128
@@ -369,6 +368,8 @@
             device_id=device, device_id_type=FAR,
         )
 
+    far_w, far_g = far, far
+
     def z_at(dz):
         return lax.rem(z + zs - dz, zs)
 
@@ -385,17 +386,22 @@
     pl.semaphore_wait(barrier, len(everyone))
 
     class Gather:
-        def __init__(self, ref, r, columns, base):
-            self.ref, self.r, self.columns, self.base = ref, r, columns, base
+        def __init__(self, ref, r, columns, base, own=None, columns_at=None):
+            self.ref, self.r, self.columns, self.base, self.own = ref, r, columns, base, own
+            self.columns_at = columns_at
 
         def part(self, zz, yy, cc):
             return self.ref.at[zz, block_rows(self.r, yy, cc), self.columns]
 
-        def layer(self, yy, cc):
-            return self.ref.at[:, block_rows(self.r, yy, cc), self.columns]
+        def layer(self, yy, cc, columns=None):
+            columns = self.columns if columns is None else columns
+            return self.ref.at[:, block_rows(self.r, yy, cc), columns]
 
         def z_copy(self, dz):
-            return far(self.part(z, y, c), self.part(z, y, c), self.base + dz - 1, z_peers[dz - 1])
+            columns = self.columns if self.columns_at is None else self.columns_at(dz)
+            there = self.ref.at[z, block_rows(self.r, y, c), columns]
+            here = there if self.own is None else self.own.at[:, columns]
+            return far_w(here, there, self.base + dz - 1, z_peers[dz - 1])
 
         def z_start(self):
             for dz in range(1, zs):
@@ -404,16 +410,18 @@
         def z_wait(self):
             for dz in range(1, zs):
                 block = self.part(z_at(dz), y, c)
-                far(block, block, self.base + dz - 1, z_peers[dz - 1]).wait_recv()
+                far_w(block, block, self.base + dz - 1, z_peers[dz - 1]).wait_recv()
 
         def y_copy(self, yy):
-            return far(self.layer(yy, c), self.layer(yy, c), self.base + zs - 1, y_peer)
+            return far_w(self.layer(yy, c), self.layer(yy, c), self.base + zs - 1, y_peer)
 
         def c_copy(self, yy, cc, other):
-            return far(self.layer(yy, cc), self.layer(yy, cc), self.base + zs + other, c_peer)
-
-        def relay(self):
+            return far_w(self.layer(yy, cc), self.layer(yy, cc), self.base + zs + other, c_peer)
+
+        def relay(self, *following):
             self.z_wait()
+            for other in following:
+                other.z_start()
             self.y_copy(y).start()
             self.c_copy(y, c, 0).start()
 
@@ -432,17 +440,76 @@
             self.c_copy(y, c, 0).wait_send()
             self.c_copy(1 - y, c, 1).wait_send()
 
+    class GatherHalf(Gather):
+        def __init__(self, ref, r, columns, others, base, own):
+            super().__init__(ref, r, columns, base, own)
+            self.others = others
+
+        def x_copy(self, yy, columns, other):
+            block = self.layer(yy, c, columns)
+            return far_w(block, block, self.base + zs + 2 + other, x_peer)
+
+        def c_other(self, yy, cc, other):
+            block = self.layer(yy, cc, self.others)
+            return far_w(block, block, self.base + zs + 4 + other, c_peer)
+
+        def push_x(self):
+            self.x_copy(y, self.columns, 0).start()
+
+        def relay_y(self):
+            super().relay_y()
+            self.x_copy(1 - y, self.columns, 1).start()
+
+        def relay_x(self):
+            self.x_copy(y, self.others, 0).wait_recv()
+            self.c_other(y, c, 0).start()
+            self.x_copy(1 - y, self.others, 1).wait_recv()
+            self.c_other(1 - y, c, 1).start()
+
+        def finish(self):
+            super().finish()
+            self.c_other(y, 1 - c, 0).wait_recv()
+            self.c_other(1 - y, 1 - c, 1).wait_recv()
+
+        def sent(self):
+            super().sent()
+            self.x_copy(y, self.columns, 0).wait_send()
+            self.x_copy(1 - y, self.columns, 1).wait_send()
+            self.c_other(y, c, 0).wait_send()
+            self.c_other(1 - y, c, 1).wait_send()
+
     steps = zs + 2
     base_q = number.take(pairs * steps)
 
     def gather_q(p):
         return Gather(wq, rq, pl.ds(pl.multiple_of(p * local, 128), local), base_q + p * steps)
 
-    gather_o = Gather(wo, rq, pl.ds(0, width), number.take(steps))
-    halves_u = 2
-    span_u = wu.shape[2] // halves_u
-    gather_u = [Gather(wu, rq, pl.ds(i * span_u, span_u), number.take(steps)) for i in range(halves_u)]
-    gather_d = Gather(wd, rd, pl.ds(0, width), number.take(steps))
+    gather_o = Gather(wo, rq, pl.ds(0, width), number.take(steps), own_o)
+    base_gu = number.take(tiles * steps)
+
+    def tile_lanes(t):
+        return pl.ds(pl.multiple_of(t * tile, 128), tile)
+
+    def turn(i, zz):
+        return lax.rem(zz + i + 1, zs)
+
+    def gather_u(i):
+        return Gather(
+            wu, rq, tile_lanes(turn(i, z)), base_gu + i * steps, own_u,
+            lambda dz: tile_lanes(turn(i, lax.rem(z + dz, zs))),
+        )
+
+    cuts = local // 128 - 1
+    base_gd = number.take(cuts * (zs + 6))
+    base_gw = number.take(2 * steps)
+
+    def gather_d(i):
+        mine = pl.ds(pl.multiple_of(s * local + i * 128, 128), 128)
+        others = pl.ds(pl.multiple_of((1 - s) * local + i * 128, 128), 128)
+        return GatherHalf(wd, rd, mine, others, base_gd + i * (zs + 6), own_d)
+
+    def gather_w(i):
+        return Gather(wd, rd, pl.ds(i * local + cuts * 128, 128), base_gw + i * steps, own_d)
 
     near_q = []
     for p in range(pairs):
@@ -462,13 +529,15 @@
                 own, whole.at[z, block_rows(r, y, c), :], near_sem.at[local_number.take(1)]
             )
         )
-    for copy in near_q + near_rest:
+    near_cot = pltpu.make_async_copy(cot, gout, near_sem.at[local_number.take(1)])
+    near_tok = pltpu.make_async_copy(tok_own, tok, near_sem.at[local_number.take(1)])
+    for copy in near_q + [near_tok] + near_rest + [near_cot]:
         copy.start()
 
     base_e = number.take(zs + 1)
     for dz in range(1, zs):
         far(table, e_z.at[dz - 1], base_e + dz - 1, z_peers[dz - 1]).start()
-    send_tok = far(tok, tok_far, number.take(1), x_peer)
+    send_tok = far(tok_own, tok_far, number.take(1), x_peer)
     send_tok.start()
     for copy in near_q:
         copy.wait()
@@ -483,6 +552,7 @@
     e_own[0] = total.astype(BF)
     y_table = far(e_own.at[0], e_y, base_e + zs - 1, y_peer)
     y_table.start()
+    gather_q(0).relay(gather_o)
 
     ends = []
     end = jnp.int32(0)
@@ -501,6 +571,7 @@
     e_own[1] = total.astype(BF)
     c_table = far(e_own.at[1], e_c, base_e + zs, c_peer)
     c_table.start()
+    gather_q(1).relay(gather_u(0))
     c_table.wait_recv()
     total = total + e_c[...].astype(F32)
     for i in range(TABLE):
@@ -517,18 +588,8 @@
 
         loop(rows // 128, body)
 
+    near_tok.wait()
     first_norm(tok, s * rows)
-
-    for p in range(pairs):
-        gather_q(p).relay()
-    for copy in near_rest:
-        copy.wait()
-    gather_o.z_start()
-    for part in gather_u:
-        part.z_start()
-
-    send_tok.wait_recv()
-    first_norm(tok_far, (1 - s) * rows)
 
     base_mixed = number.take(pairs)
     near_mixed = local_number.take(pairs)
@@ -568,6 +629,17 @@
         return jnp.where(ok, raw, MASKED)
 
     scale = HEAD_DIM ** (-0.5)
+
+    def pass_on(k):
+        @pl.when(k == 0)
+        def _():
+            gather_u(0).relay(gather_d(0))
+            gather_o.relay_y()
+
+        @pl.when(k == 3)
+        def _():
+            gather_u(1).relay(gather_d(1))
+            gather_u(0).relay_y()
 
     def attend(p):
         def head(h):
@@ -593,6 +665,7 @@
                     )
                 o_t[half, qi * side : (qi + 1) * side] = gathered / amount
                 lse[p, h, :, qi * side : (qi + 1) * side] = top + jnp.log(amount)
+            pass_on(p * 2 + h)
 
         loop(2, head)
         here = pl.ds(pl.multiple_of(p * 128, 128), 128)
@@ -600,44 +673,50 @@
             at = slice(qi * side, (qi + 1) * side)
             mixed_near[at, here] = o_t[:, at].T.astype(BF)
 
-    def project(p):
+    def project(p, at_row):
         zero = jnp.zeros((1, 128), F32)
         there = pl.ds(pl.multiple_of(s * local + p * 128, 128), 128)
         bias = jnp.concatenate([vec[BIAS_Q, :, there], zero, vec[BIAS_V, :, there]], axis=1)
         weight = flat(wq[:, :, pl.ds(pl.multiple_of(p * local, 128), local)])
 
         def body(i):
-            at = pl.ds(pl.multiple_of(i * side, side), side)
+            at = pl.ds(pl.multiple_of(at_row + i * side, side), side)
             value = (mul(first[at, :], weight) + bias).astype(BF)
             qkv[at, pl.ds(pl.multiple_of(p * local, 128), local)] = value
             k_t[p, :, at] = value[:, 128:256].T
             v_t[p, :, at] = value[:, 256:384].T
 
-        loop(blocks, body)
+        loop(rows // side, body)
+
+    gather_q(0).relay_y()
+    gather_q(2).relay(gather_u(1))
+    gather_q(0).finish()
+    project(0, s * rows)
+    gather_q(1).relay_y()
+    for copy in near_rest:
+        copy.wait()
+    gather_o.relay(gather_u(2))
+    gather_q(2).relay_y()
+    send_tok.wait_recv()
+    first_norm(tok_far, (1 - s) * rows)
 
     def pair_forward(p):
-        gather_q(p).relay_y()
-        gather_q(p).finish()
-        project(p)
+        @pl.when(p > 0)
+        def _():
+            gather_q(p).finish()
+            project(p, s * rows)
+
+        project(p, (1 - s) * rows)
         attend(p)
         send_mixed(p).start()
         keep_mixed(p).start()
 
-        @pl.when(p == 0)
-        def _():
-            gather_o.relay()
-            gather_u[0].relay()
-
-        @pl.when(p == 1)
-        def _():
-            gather_u[1].relay()
-            gather_d.z_start()
-
     loop(pairs, pair_forward)
-
-    gather_o.relay_y()
-    gather_u[0].relay_y()
+    gather_u(2).relay(gather_u(3))
+    gather_u(1).relay_y()
+
     gather_o.finish()
+    near_cot.wait()
     for p in range(pairs):
         keep_mixed(p).wait()
     for p in range(pairs):
@@ -653,203 +732,269 @@
         mixed_t[:, at] = near.T
         value = tok[at, :].astype(F32) + mul(near, flat(wo[...])) + vec[BIAS_OUT]
         middle[at, :] = value
-        result[at, :] = value + vec[BIAS_DOWN]
         scaled, unused = normed(value)
         rounded = (scaled * vec[GAIN_2] + vec[SHIFT_2]).astype(BF)
         second[at, :] = rounded
         second_t[:, at] = rounded.T
+        gtok[at, :] = jnp.zeros((128, width), F32)
         spot = s * rows + i * 128 + lax.broadcasted_iota(jnp.int32, (128, width), 0)
-        gout[at, :] = jnp.where(spot < last_valid, cot[at, :].astype(F32), 0.0).astype(BF)
-        gtok[at, :] = jnp.zeros((128, width), F32)
+        gout[at, :] = jnp.where(spot < last_valid, gout[at, :].astype(F32), 0.0).astype(BF)
 
     loop(rows // 128, project_out)
-
-    gather_u[1].relay_y()
-    gather_d.relay()
-    gather_u[0].finish()
-    gather_u[1].finish()
-    gather_d.relay_y()
-    gather_d.finish()
-    for part in gather_u + [gather_d]:
-        part.sent()
+    gather_d(0).relay(gather_w(0))
+    gather_d(0).push_x()
+
 
     base_sib = number.take(tiles * 4)
-    base_ys = number.take(tiles * 2)
+    base_dx = number.take(tiles * 2)
+    base_uy = number.take(tiles)
     base_zd = number.take(zs - 1)
     base_zu = number.take(tiles * (zs - 1))
     base_xs = number.take(2)
-
-    def tile_lanes(t):
-        return pl.ds(pl.multiple_of(t * tile, 128), tile)
+    mine = pl.ds(pl.multiple_of(s * local, 128), local)
+    others = pl.ds(pl.multiple_of((1 - s) * local, 128), local)
+
+    def rows_y(r, yy):
+        return pl.ds(pl.multiple_of(yy * r, r), r)
 
     def sib_d(t, yy):
-        return far(
-            wd.at[t, block_rows(rd, yy, 1 - c), :],
-            r1_d.at[t, pl.ds(pl.multiple_of(yy * rd, rd), rd), :],
+        return far_g(
+            gwd.at[t, block_rows(rd, yy, 1 - c), :], r1_d.at[t, rows_y(rd, yy), :],
             base_sib + t * 4 + yy, c_peer,
         )
 
+    def sib_start_d(t):
+        for yy in range(2):
+            sib_d(t, yy).start()
+
+    def x_d(t):
+        return far_g(r1_d.at[t, :, others], rx_d.at[t], base_dx + t * 2, x_peer)
+
+    def x_start_d(t):
+        for yy in range(2):
+            sib_d(t, yy).wait_recv()
+            at = rows_y(rd, yy)
+            r1_d[t, at, :] = (
+                r1_d[t, at, :].astype(F32) + gwd[t, block_rows(rd, yy, c), :].astype(F32)
+            ).astype(BF)
+        x_d(t).start()
+
+    def y_d(t):
+        return far_g(rx_d.at[t, rows_y(rd, 1 - y), :], ry_d.at[t], base_dx + t * 2 + 1, y_peer)
+
+    def y_start_d(t):
+        x_d(t).wait_recv()
+        rx_d[t] = (rx_d[t].astype(F32) + r1_d[t, :, mine].astype(F32)).astype(BF)
+        y_d(t).start()
+
+    def z_d(t, dz):
+        return far_g(ry_d.at[t], rz_d.at[dz - 1], base_zd + dz - 1, (t * 4 + y * 2 + c, s))
+
+    def z_start_d(t):
+        y_d(t).wait_recv()
+        ry_d[t] = (ry_d[t].astype(F32) + rx_d[t, rows_y(rd, y), :].astype(F32)).astype(BF)
+        dz = lax.rem(t + zs - z, zs)
+
+        @pl.when(dz > 0)
+        def _():
+            z_d(t, dz).start()
+
     def sib_u(t, yy):
-        return far(
+        return far_g(
             wu.at[:, block_rows(rq, yy, 1 - c), tile_lanes(t)],
-            r1_u.at[:, pl.ds(pl.multiple_of(yy * rq, rq), rq), tile_lanes(t)],
+            r1_u.at[:, rows_y(rq, yy), tile_lanes(t)],
             base_sib + t * 4 + 2 + yy, c_peer,
         )
 
-    def sib_start(t):
+    def sib_start_u(t):
         for yy in (1 - y, y):
-            sib_d(t, yy).start()
             sib_u(t, yy).start()
 
-    def y_d(t):
-        return far(
-            r1_d.at[t, pl.ds(pl.multiple_of((1 - y) * rd, rd), rd), :], r2_d.at[t],
-            base_ys + t * 2, y_peer,
-        )
-
     def y_u(t):
-        return far(
-            r1_u.at[:, pl.ds(pl.multiple_of((1 - y) * rq, rq), rq), tile_lanes(t)],
-            r2_u.at[:, :, tile_lanes(t)], base_ys + t * 2 + 1, y_peer,
-        )
-
-    def y_start(t):
+        return far_g(
+            r1_u.at[:, rows_y(rq, 1 - y), tile_lanes(t)], r2_u.at[:, :, tile_lanes(t)],
+            base_uy + t, y_peer,
+        )
+
+    def y_start_u(t):
         yy = 1 - y
-        sib_d(t, yy).wait_recv()
-        at = pl.ds(pl.multiple_of(yy * rd, rd), rd)
-        r1_d[t, at, :] = (
-            r1_d[t, at, :].astype(F32) + wd[t, block_rows(rd, yy, c), :].astype(F32)
-        ).astype(BF)
         sib_u(t, yy).wait_recv()
-        at = pl.ds(pl.multiple_of(yy * rq, rq), rq)
+        at = rows_y(rq, yy)
         for zz in range(zs):
             r1_u[zz, at, tile_lanes(t)] = (
                 r1_u[zz, at, tile_lanes(t)].astype(F32)
                 + wu[zz, block_rows(rq, yy, c), tile_lanes(t)].astype(F32)
             ).astype(BF)
-        y_d(t).start()
         y_u(t).start()
 
-    def z_d(t, dz):
-        return far(r2_d.at[t], r3_d.at[dz - 1], base_zd + dz - 1, (t * 4 + y * 2 + c, s))
-
     def z_u(t, dz):
-        return far(
+        return far_g(
             r2_u.at[lax.rem(z + dz, zs), :, tile_lanes(t)], r3_u.at[dz - 1, :, tile_lanes(t)],
             base_zu + t * (zs - 1) + dz - 1, z_peers[dz - 1],
         )
 
-    def z_start(t):
-        sib_d(t, y).wait_recv()
-        y_d(t).wait_recv()
-        at = pl.ds(pl.multiple_of(y * rd, rd), rd)
-        r2_d[t] = (
-            r2_d[t].astype(F32)
-            + r1_d[t, at, :].astype(F32)
-            + wd[t, block_rows(rd, y, c), :].astype(F32)
-        ).astype(BF)
+    def z_start_u(t):
         sib_u(t, y).wait_recv()
         y_u(t).wait_recv()
-        at = pl.ds(pl.multiple_of(y * rq, rq), rq)
+        at = rows_y(rq, y)
         for zz in range(zs):
             r2_u[zz, :, tile_lanes(t)] = (
                 r2_u[zz, :, tile_lanes(t)].astype(F32)
                 + r1_u[zz, at, tile_lanes(t)].astype(F32)
                 + wu[zz, block_rows(rq, y, c), tile_lanes(t)].astype(F32)
             ).astype(BF)
-        dz = lax.rem(t + zs - z, zs)
-
-        @pl.when(dz > 0)
-        def _():
-            z_d(t, dz).start()
-
         for step in range(1, zs):
             z_u(t, step).start()
 
     sub = 256
 
-    def feed(t):
+    def pass_up(k):
+        @pl.when(k == 1)
+        def _():
+            gather_u(2).relay_y()
+
+        @pl.when(k == 2)
+        def _():
+            gather_d(1).relay(gather_w(1))
+            gather_d(1).push_x()
+
+        @pl.when(k == 3)
+        def _():
+            gather_d(0).relay_y()
+
+        @pl.when(k == 4)
+        def _():
+            x_start_d(turn(0, z))
+
+        @pl.when(k == 5)
+        def _():
+            gather_u(3).relay()
+
+        @pl.when(k == 6)
+        def _():
+            gather_d(1).relay_y()
+            gather_d(0).relay_x()
+
+        @pl.when(k == 7)
+        def _():
+            gather_w(0).relay()
+
+        @pl.when(k == 8)
+        def _():
+            gather_u(3).relay_y()
+
+        @pl.when(k == 9)
+        def _():
+            gather_w(1).relay()
+            gather_d(1).relay_x()
+
+        @pl.when(k == 10)
+        def _():
+            gather_w(0).relay_y()
+            x_start_d(turn(1, z))
+
+    def feed(i):
+        t = turn(i, z)
+        gather_u(i).finish()
+
         def part(u):
             at = pl.ds(pl.multiple_of(t * tile + u * sub, 128), sub)
             near = pl.ds(pl.multiple_of(u * sub, sub), sub)
             pre = mul(second[...], flat(wu[:, :, at])) + vec[BIAS_UP + t, :, near]
             bent = jnp.tanh(SLOPE * (pre + CUBIC * pre * pre * pre))
             value = (0.5 * pre * (1.0 + bent)).astype(BF)
-            slope = 0.5 * (1.0 + bent) + 0.5 * pre * (1.0 - bent * bent) * SLOPE * (
+            bend = 0.5 * (1.0 + bent) + 0.5 * pre * (1.0 - bent * bent) * SLOPE * (
                 1.0 + 3.0 * CUBIC * pre * pre
             )
-            hidden[:, near] = value
+            hidden[:, at] = value
             hidden_t[near, :] = value.T
-            grad = (mul_nt(gout[...], wd[t, near, :]) * slope).astype(BF)
-            gpre[:, near] = grad
-            gvec[BIAS_UP + t, :, near] = column_sum(grad.astype(F32))
+            slope[:, at] = bend.astype(BF)
+            pass_up(i * (tile // sub) + u)
 
         loop(tile // sub, part)
 
+        def weigh(m):
+            at = pl.ds(pl.multiple_of(m * rd, rd), rd)
+            gwd[t, at, :] = mul(hidden_t[at, :], gout[...]).astype(BF)
+
+        loop(4, weigh)
+        sib_start_d(t)
+
+    loop(tiles, feed)
+    y_start_d(turn(0, z))
+    x_start_d(turn(2, z))
+    gather_w(1).relay_y()
+    for i in range(cuts):
+        gather_d(i).finish()
+    for i in range(2):
+        gather_w(i).finish()
+
+    def slopes_back(i):
+        at = pl.ds(pl.multiple_of(i * sub, sub), sub)
+        t = lax.div(i, tile // sub)
+        near = pl.ds(pl.multiple_of((i - t * (tile // sub)) * sub, sub), sub)
+        grad = (mul_nt(gout[...], wd[t, near, :]) * slope[:, at].astype(F32)).astype(BF)
+        slope[:, at] = grad
+        gvec[BIAS_UP + t, :, near] = column_sum(grad.astype(F32))
+
+    loop(tiles * (tile // sub), slopes_back)
+    y_start_d(turn(1, z))
+    x_start_d(z)
+    z_start_d(turn(0, z))
+
+    def grow(t):
         def add(i):
             at = pl.ds(pl.multiple_of(i * side, side), side)
-            result[at, :] += mul(hidden[at, :], wd[t])
-            gtok[at, :] += mul_nt(gpre[at, :], flat(wu[:, :, tile_lanes(t)]))
+            gtok[at, :] += mul_nt(slope[at, tile_lanes(t)], flat(wu[:, :, tile_lanes(t)]))
 
         loop(rows // side, add)
 
-        def weigh(m):
-            at = pl.ds(pl.multiple_of(m * rd, rd), rd)
-            wd[t, at, :] = mul(hidden_t[at, :], gout[...]).astype(BF)
-
-        loop(4, weigh)
-
-        def weigh_up(m):
-            at = pl.ds(pl.multiple_of(m * 4 * rq, 4 * rq), 4 * rq)
-            wu[m, :, tile_lanes(t)] = mul(second_t[at, :], gpre[...]).astype(BF)
-
-        loop(zs, weigh_up)
-        sib_start(t)
-
-        @pl.when(t > 0)
-        def _():
-            y_start(t - 1)
-
-    loop(tiles, feed)
+    loop(tiles, grow)
 
     for row in (BIAS_Q, BIAS_V, BIAS_OUT, BIAS_DOWN, GAIN_1, SHIFT_1, GAIN_2, SHIFT_2):
         gvec[row] = jnp.zeros((1, width), F32)
     for row in range(BIAS_UP + tiles, TABLE):
         gvec[row] = jnp.zeros((1, width), F32)
+    gattn = mixed
+    gmix = second
 
     def middle_back(i):
         at = pl.ds(pl.multiple_of(i * 128, 128), 128)
+        grad = gtok[at, :]
         scaled, inverse = normed(middle[at, :])
-        grad = gtok[at, :]
         ahead = gout[at, :].astype(F32)
         gvec[GAIN_2] += column_sum(grad * scaled)
         gvec[SHIFT_2] += column_sum(grad)
         gvec[BIAS_DOWN] += column_sum(ahead)
         total = ahead + normed_back(grad, scaled, inverse, vec[GAIN_2])
-        middle[at, :] = total
+        gtok[at, :] = total
         rounded = total.astype(BF)
         gattn[at, :] = rounded
         gvec[BIAS_OUT] += column_sum(rounded.astype(F32))
         gmix[at, :] = mul_nt(rounded, flat(wo[...])).astype(BF)
-        spot = s * rows + i * 128 + lax.broadcasted_iota(jnp.int32, (128, width), 0)
-        out[at, :] = jnp.where(spot < last_valid, result[at, :], 0.0).astype(BF)
 
     loop(rows // 128, middle_back)
 
-    slot_gmix = number.take(1)
-    send_gmix = far(
-        gmix.at[:, pl.ds(pl.multiple_of((1 - s) * local, 128), local)],
-        gmix_head.at[pl.ds(pl.multiple_of(s * rows, 128), rows), :],
-        slot_gmix, x_peer,
-    )
+    base_gmix = number.take(pairs)
+    near_gmix = local_number.take(1)
+    here_rows = pl.ds(pl.multiple_of(s * rows, 128), rows)
+    there_rows = pl.ds(pl.multiple_of((1 - s) * rows, 128), rows)
+
+    def send_gmix(p):
+        lanes_p = pl.ds(pl.multiple_of((1 - s) * local + p * 128, 128), 128)
+        at = pl.ds(pl.multiple_of(p * 128, 128), 128)
+        return far(gmix.at[:, lanes_p], gmix_head.at[here_rows, at], base_gmix + p, x_peer)
+
+    def take_gmix(p):
+        at = pl.ds(pl.multiple_of(p * 128, 128), 128)
+        return far(gmix.at[:, pl.ds(0, 128)], gmix_head.at[there_rows, at], base_gmix + p, x_peer)
+
     keep_gmix = pltpu.make_async_copy(
-        gmix.at[:, pl.ds(pl.multiple_of(s * local, 128), local)],
-        gmix_head.at[pl.ds(pl.multiple_of(s * rows, 128), rows), :],
-        near_sem.at[local_number.take(1)],
-    )
-    send_gmix.start()
+        gmix.at[:, mine], gmix_head.at[here_rows, :], near_sem.at[near_gmix]
+    )
+    for p in range(pairs):
+        send_gmix(p).start()
     keep_gmix.start()
-    y_start(tiles - 1)
 
     gather_o.sent()
 
@@ -858,6 +1003,10 @@
         wo[m] = mul(mixed_t[at, :], gattn[...]).astype(BF)
 
     loop(zs, weigh_out)
+    y_start_d(turn(2, z))
+    z_start_d(turn(1, z))
+    for t in range(tiles):
+        gather_u(t).sent()
 
     class Spread:
         def __init__(self, ref, columns, r1, r2, r3, base):
@@ -865,7 +1014,7 @@
             self.base = base
 
         def sib(self, yy):
-            return far(
+            return far_g(
                 self.ref.at[:, block_rows(rq, yy, 1 - c), self.columns],
                 self.r1.at[:, pl.ds(pl.multiple_of(yy * rq, rq), rq), self.columns],
                 self.base + yy, c_peer,
@@ -876,7 +1025,7 @@
             self.sib(y).start()
 
         def along_y(self):
-            return far(
+            return far_g(
                 self.r1.at[:, pl.ds(pl.multiple_of((1 - y) * rq, rq), rq), self.columns],
                 self.r2.at[:, :, self.columns], self.base + 2, y_peer,
             )
@@ -892,7 +1041,7 @@
             self.along_y().start()
 
         def along_z(self, dz):
-            return far(
+            return far_g(
                 self.r2.at[lax.rem(z + dz, zs), :, self.columns],
                 self.r3.at[dz - 1, :, self.columns], self.base + 2 + dz, z_peers[dz - 1],
             )
@@ -935,14 +1084,85 @@
         )
 
     sum_o.sib_start()
-    send_gmix.wait_send()
+
+    def weigh_up_tile(t):
+        def weigh_up(m):
+            at = pl.ds(pl.multiple_of(m * 4 * rq, 4 * rq), 4 * rq)
+            wu[m, :, tile_lanes(t)] = mul(second_t[at, :], slope[:, tile_lanes(t)]).astype(BF)
+
+        loop(zs, weigh_up)
+        sib_start_u(t)
+
+        @pl.when(t == 0)
+        def _():
+            sum_o.y_start()
+
+        @pl.when(t > 0)
+        def _():
+            y_start_u(t - 1)
+
+        @pl.when(t == 2)
+        def _():
+            y_start_d(z)
+            z_start_d(turn(2, z))
+
+    loop(tiles, weigh_up_tile)
+    y_start_u(tiles - 1)
+
+    def fall(t):
+        def add(i):
+            at = pl.ds(pl.multiple_of(i * side, side), side)
+            middle[at, :] += mul(hidden[at, tile_lanes(t)], wd[t])
+
+        loop(rows // side, add)
+
+    loop(tiles, fall)
+
+    def finish_out(i):
+        at = pl.ds(pl.multiple_of(i * 128, 128), 128)
+        value = middle[at, :] + vec[BIAS_DOWN]
+        spot = s * rows + i * 128 + lax.broadcasted_iota(jnp.int32, (128, width), 0)
+        out[at, :] = jnp.where(spot < last_valid, value, 0.0).astype(BF)
+
+    loop(rows // 128, finish_out)
     keep_gmix.wait()
-    far(
-        gmix.at[:, pl.ds(0, local)],
-        gmix_head.at[pl.ds(pl.multiple_of((1 - s) * rows, 128), rows), :],
-        slot_gmix, x_peer,
-    ).wait_recv()
-    sum_o.y_start()
+
+    xd = far_g(r5_d.at[s], r5_d.at[s], base_xs, x_peer)
+    xo = far_g(r5_o.at[0], r5_o.at[1], number.take(1), x_peer)
+
+    def finish_d():
+        total = ry_d[z].astype(F32)
+        for dz in range(1, zs):
+            far_g(ry_d.at[0], rz_d.at[dz - 1], base_zd + dz - 1, z_peers[dz - 1]).wait_recv()
+            total = total + rz_d[dz - 1].astype(F32)
+        r5_d[s] = total.astype(BF)
+        xd.start()
+
+    def finish_o():
+        r5_o[0] = sum_o.z_finish().astype(BF)
+        xo.start()
+
+    def serve(k):
+        @pl.when(k == 0)
+        def _():
+            sum_o.z_start()
+
+        @pl.when(k == 2)
+        def _():
+            z_start_u(0)
+
+        @pl.when(k == 3)
+        def _():
+            z_start_u(1)
+            finish_o()
+
+        @pl.when(k == 4)
+        def _():
+            z_start_u(2)
+
+        @pl.when(k == 5)
+        def _():
+            z_start_d(z)
 
     def attend_back(p):
         dk[...] = jnp.zeros_like(dk)
@@ -973,27 +1193,28 @@
                     dk[there, :] += mul(bend, query)
                     dv[there, :] += mul(weights[j].astype(BF), grad)
                     total = total + mul(k_t[p, half, there], bend)
-                dq_t[half, at] = total * scale
+                o_t[half, at] = total * scale
+            serve(p * 2 + h)
 
         loop(2, head)
         for qi in range(blocks):
             at = slice(qi * side, (qi + 1) * side)
-            gqkv[at, lanes(p, 0)] = dq_t[:, at].T.astype(BF)
-            gqkv[at, lanes(p, 1)] = dk[at, :].astype(BF)
-            gqkv[at, lanes(p, 2)] = dv[at, :].astype(BF)
+            qkv[at, lanes(p, 0)] = o_t[:, at].T.astype(BF)
+            qkv[at, lanes(p, 1)] = dk[at, :].astype(BF)
+            qkv[at, lanes(p, 2)] = dv[at, :].astype(BF)
         own = pl.ds(pl.multiple_of(s * local + p * 128, 128), 128)
-        gvec[BIAS_Q, :, own] = column_sum(gqkv[:, lanes(p, 0)].astype(F32))
-        gvec[BIAS_V, :, own] = column_sum(gqkv[:, lanes(p, 2)].astype(F32))
+        gvec[BIAS_Q, :, own] = column_sum(qkv[:, lanes(p, 0)].astype(F32))
+        gvec[BIAS_V, :, own] = column_sum(qkv[:, lanes(p, 2)].astype(F32))
         both = pl.ds(pl.multiple_of(p * local, 128), local)
 
         def weigh(m):
             at = pl.ds(pl.multiple_of(m * 4 * rq, 4 * rq), 4 * rq)
-            gwq[m, :, both] = mul(first_t[at, :], gqkv[:, both]).astype(BF)
+            gwq[m, :, both] = mul(first_t[at, :], qkv[:, both]).astype(BF)
 
         loop(zs, weigh)
 
     def pair_back(p):
-        z_start(p)
+        take_gmix(p).wait_recv()
         attend_back(p)
         sum_q(p).sib_start()
 
@@ -1007,11 +1228,12 @@
 
     def send_gf(i):
         at = pl.ds(pl.multiple_of(i * side, side), side)
-        return far(gf_send.at[at, :], gf_recv.at[at, :], base_gf + i, x_peer)
+        there = pl.ds(pl.multiple_of(rows + i * side, side), side)
+        return far(first.at[at, :], first.at[there, :], base_gf + i, x_peer)
 
     def first_back(i, source, at):
         there = pl.ds(pl.multiple_of(at + i * side, side), side)
-        grad = mul_nt(gqkv[there, :], flat(wq[...]))
+        grad = mul_nt(qkv[there, :], flat(wq[...]))
         scaled, unused = normed(source[pl.ds(pl.multiple_of(i * side, side), side), :].astype(F32))
         gvec[GAIN_1] += column_sum(grad * scaled)
         gvec[SHIFT_1] += column_sum(grad)
@@ -1019,22 +1241,21 @@
 
     def away(i):
         grad = first_back(i, tok_far, (1 - s) * rows)
-        gf_send[pl.ds(pl.multiple_of(i * side, side), side), :] = grad.astype(BF)
+        first[pl.ds(pl.multiple_of(i * side, side), side), :] = grad.astype(BF)
         send_gf(i).start()
 
     loop(rows // side, away)
     sum_q(pairs - 1).y_start()
+    z_start_u(3)
 
     def stay(i):
-        gtok[pl.ds(pl.multiple_of(i * side, side), side), :] = first_back(i, tok, s * rows)
+        middle[pl.ds(pl.multiple_of(i * side, side), side), :] = first_back(i, tok, s * rows)
 
     loop(rows // side, stay)
 
     base_v = number.take(zs + 2)
     for dz in range(1, zs):
         far(gvec, v_z.at[dz - 1], base_v + dz - 1, z_peers[dz - 1]).start()
-    z_start(tiles - 1)
-    sum_o.z_start()
     for dz in range(1, zs):
         far(gvec, v_z.at[dz - 1], base_v + dz - 1, z_peers[dz - 1]).wait_recv()
     for i in range(TABLE):
@@ -1055,13 +1276,7 @@
     vx = far(v_sum.at[2], v_x, base_v + zs + 1, x_peer)
     vx.start()
 
-    total = r2_d[z].astype(F32)
-    for dz in range(1, zs):
-        far(r2_d.at[0], r3_d.at[dz - 1], base_zd + dz - 1, z_peers[dz - 1]).wait_recv()
-        total = total + r3_d[dz - 1].astype(F32)
-    r5_d[0] = total.astype(BF)
-    xd = far(r5_d.at[0], r5_d.at[1], base_xs, x_peer)
-    xd.start()
+    finish_d()
     for t in range(tiles):
         for dz in range(1, zs):
             z_u(t, dz).wait_recv()
@@ -1073,15 +1288,12 @@
         r5_u[0, :, tile_lanes(t)] = total.astype(BF)
 
     loop(tiles, finish_u)
-    xu = far(r5_u.at[0], r5_u.at[1], base_xs + 1, x_peer)
+    xu = far_g(r5_u.at[0], r5_u.at[1], base_xs + 1, x_peer)
     xu.start()
-    r5_o[0] = sum_o.z_finish().astype(BF)
-    xo = far(r5_o.at[0], r5_o.at[1], number.take(1), x_peer)
-    xo.start()
     for p in range(pairs):
         r5_q[s, :, p * local : (p + 1) * local] = sum_q(p).z_finish().astype(BF)
     slot_q = number.take(1)
-    xq = far(r5_q.at[s], r5_q.at[s], slot_q, x_peer)
+    xq = far_g(r5_q.at[s], r5_q.at[s], slot_q, x_peer)
     xq.start()
 
     for i in range(rows // side):
@@ -1090,15 +1302,17 @@
     def last(i):
         at = pl.ds(pl.multiple_of(i * 128, 128), 128)
         scaled, inverse = normed(tok[at, :].astype(F32))
-        grad = gtok[at, :] + gf_recv[at, :].astype(F32)
-        gtok[at, :] = middle[at, :] + normed_back(grad, scaled, inverse, vec[GAIN_1])
+        there = pl.ds(pl.multiple_of(rows + i * 128, 128), 128)
+        grad = middle[at, :] + first[there, :].astype(F32)
+        gtok[at, :] = gtok[at, :] + normed_back(grad, scaled, inverse, vec[GAIN_1])
 
     loop(rows // 128, last)
 
     vx.wait_recv()
     out_v[...] = v_sum[2] + v_x[...]
-    xd.wait_recv()
-    out_d[...] = r5_d[0].astype(F32) + r5_d[1].astype(F32)
+    far_g(r5_d.at[1 - s], r5_d.at[1 - s], base_xs, x_peer).wait_recv()
+    for half in range(2):
+        out_d[:, half * local : (half + 1) * local] = r5_d[half].astype(F32)
     xu.wait_recv()
 
     def store_u(t):
@@ -1107,7 +1321,7 @@
     loop(tiles, store_u)
     xo.wait_recv()
     out_o[...] = r5_o[0].astype(F32) + r5_o[1].astype(F32)
-    far(r5_q.at[1 - s], r5_q.at[1 - s], slot_q, x_peer).wait_recv()
+    far_g(r5_q.at[1 - s], r5_q.at[1 - s], slot_q, x_peer).wait_recv()
     for half in range(2):
         for p in range(pairs):
             for part in range(3):
@@ -1119,7 +1333,7 @@
     for dz in range(1, zs):
         far(table, e_z.at[dz - 1], base_e + dz - 1, z_peers[dz - 1]).wait_send()
         far(gvec, v_z.at[dz - 1], base_v + dz - 1, z_peers[dz - 1]).wait_send()
-        far(r2_d.at[0], r3_d.at[dz - 1], base_zd + dz - 1, z_peers[dz - 1]).wait_send()
+        far_g(ry_d.at[0], rz_d.at[dz - 1], base_zd + dz - 1, z_peers[dz - 1]).wait_send()
     for copy in (y_table, c_table, send_tok, vy, vc, vx, xd, xu, xo, xq):
         copy.wait_send()
     for p in range(pairs):
@@ -1127,10 +1341,17 @@
         send_mixed(p).wait_send()
         sum_q(p).sent()
     sum_o.sent()
+    for i in range(cuts):
+        gather_d(i).sent()
+    for i in range(2):
+        gather_w(i).sent()
+    for p in range(pairs):
+        send_gmix(p).wait_send()
     for t in range(tiles):
         for yy in range(2):
             sib_d(t, yy).wait_send()
             sib_u(t, yy).wait_send()
+        x_d(t).wait_send()
         y_d(t).wait_send()
         y_u(t).wait_send()
         for dz in range(1, zs):
@@ -1173,25 +1394,24 @@
 
     scratch = [
         vm((zs, 4 * rq, 3 * local)), vm((zs, 4 * rq, width)), vm((zs, 4 * rq, deep)),
-        vm((zs, 4 * rd, width)), vm((zs, 4 * rq, 3 * local)),
-        vm((rows, width)), vm((group, width)), vm((width, group)), vm((group, 3 * local)),
+        vm((zs, 4 * rd, width)), vm((zs, 4 * rq, 3 * local)), vm((zs, 4 * rd, width)),
+        vm((rows, width)), vm((rows, width)), vm((group, width)), vm((width, group)), vm((group, 3 * local)),
         vm((pairs, 128, group)), vm((pairs, 128, group)), vm((1, group), jnp.int32),
         vm((pairs, 2, 1, group), F32), vm((128, group), F32),
         vm((group, local)), vm((rows, width)), vm((width, rows)), vm((rows, width), F32),
-        vm((rows, width)), vm((width, rows)), vm((rows, width)), vm((rows, width), F32),
-        vm((rows, 4 * rd)), vm((4 * rd, rows)), vm((rows, 4 * rd)), vm((rows, width)),
-        vm((group, local)), vm((rows, width)), vm((group, 128), F32), vm((group, 128), F32),
-        vm((128, group), F32), vm((group, 3 * local)),
+        vm((rows, width)), vm((width, rows)), vm((rows, width)),
+        vm((rows, deep)), vm((4 * rd, rows)), vm((rows, deep)),
+        vm((group, local)), vm((group, 128), F32), vm((group, 128), F32),
         vm((2, TABLE, width)), vm((zs - 1, TABLE, width)), vm((TABLE, width)), vm((TABLE, width)),
         vm((TABLE, 1, width), F32), vm((TABLE, 1, width), F32), vm((zs - 1, TABLE, 1, width), F32),
         vm((TABLE, 1, width), F32), vm((TABLE, 1, width), F32), vm((TABLE, 1, width), F32),
         vm((3, TABLE, 1, width), F32),
-        vm((zs, 2 * rd, width)), vm((zs, rd, width)), vm((zs - 1, rd, width)), vm((2, rd, width)),
+        vm((zs, 2 * rd, width)), vm((zs, 2 * rd, local)), vm((zs, rd, local)),
+        vm((zs - 1, rd, local)), vm((2, rd, local)),
         vm((zs, 2 * rq, deep)), vm((zs, rq, deep)), vm((zs - 1, rq, deep)), vm((2, rq, deep)),
         vm((zs, 2 * rq, width)), vm((zs, rq, width)), vm((zs - 1, rq, width)), vm((2, rq, width)),
         vm((zs, 2 * rq, 3 * local)), vm((zs, rq, 3 * local)), vm((zs - 1, rq, 3 * local)),
         vm((2, rq, 3 * local)),
-        vm((rows, width)), vm((rows, width)),
         pltpu.SemaphoreType.DMA((NEAR_COUNT,)),
         pltpu.SemaphoreType.DMA((FAR_COUNT,)),
         pltpu.SemaphoreType.DMA((FAR_COUNT,)),
@@ -1209,7 +1429,7 @@
             jax.ShapeDtypeStruct((rd, width), F32),
             jax.ShapeDtypeStruct((TABLE, 1, width), F32),
         ),
-        in_specs=[pl.BlockSpec(memory_space=pltpu.SMEM), here, here, here, away, away, away, away],
+        in_specs=[pl.BlockSpec(memory_space=pltpu.SMEM), here, away, away, away, away, away, away],
         out_specs=[here] * 7,
         scratch_shapes=scratch,
         compiler_params=pltpu.CompilerParams(

time: 246 us -> 190 us (0.77)
  Pallas kernels: 233 us -> 179 us
    pallas_call x1, Pallas kernels: 233 us -> 179 us  [fused(): pl.pallas_call(fused_kernel, out_shape=(jax.ShapeDtypeStruct((rows, width...]
where the time goes in v2:
time: 190 us
  Pallas kernels  179 us (94%)
  local copies, waits for them, and re-layouts  10.2 us (5%)
    pallas_call x1, Pallas kernels, fused(): pl.pallas_call(fused_kernel, out_shape=(jax.ShapeDtypeStruct((rows, width...  179 us
    unnamed x16, local copies, waits for them, and re-layouts  6.4 us

profile of v2, /device:TPU:0, one launch (start us, length us, event | category | flops | bytes accessed | tf_op | source)
XLA Modules:
  0.0 190.2 jit_solution(7324245683383351106)
XLA Ops:
  0.7 0.8 stack.35
  1.5 0.7 tile.8
  2.1 0.1 broadcast_in_dim.27
  2.2 0.1 fusion.2
  2.3 0.1 tile.7
  2.5 0.6 pad_maximum_fusion.table
  3.1 178.5 %block.1 = (bf16[512,768]{1,0:T(8,128)(2,1)}, f32[512,768]{1,0:T(8,128)}, f32[48,2304]{1,0:T(8,128)}, f32[48,768]{1,0:T(8,128)}, f32[48,3072]{1,0:T(8,128)}, /*index=5*/f32[192,768]{1,0:T(8,128)}, f32[16,1,768]{2,1,0:T(1,128)}) custom-call(s32[1,6]{1,0:T(1,128)} %lengths.1, bf16[16,768]{1,0:T(8,128)(2,1)} %pad_maximum_fusion.table, ...), custom_call_target="tpu_custom_call" | custom-call | tf_op jit(solution)/shard_map/block/pallas_call | solution.py:1421
  181.6 0.0 copy-start
  181.6 0.9 fusion.15
  182.5 0.6 dynamic_slice.7
  183.2 0.6 fusion.7
  183.8 2.1 %copy.37 = bf16[512,768]{1,0:T(8,128)(2,1)} copy(bf16[512,768]{1,0:T(8,128)(2,1)} %get-tuple-element.54) | data formatting | bytes 1572864
  185.9 0.0 copy-done
  185.9 0.0 copy-start.3
  185.9 0.0 copy-start.4
  185.9 0.0 copy-start.2
  185.9 1.1 copy.38
  187.0 0.1 copy-done.3
  187.1 0.0 copy-start.1
  187.1 0.8 copy.39
  187.9 0.0 copy-done.4
  187.9 0.7 copy.40
  188.6 0.0 copy-done.2
  188.6 0.8 copy.41
  189.4 0.0 copy-done.1
  189.4 0.8 copy.42
  (5 shorter events, 0.0 us)
Async XLA Ops:
  181.6 4.2 %copy-start = (f32[512,768]{1,0:T(8,128)S(1)}, f32[512,768]{1,0:T(8,128)}, u32[]{:S(2)}) copy-start(f32[512,768]{1,0:T(8,128)} %get-tuple-element.55) | copy-start | bytes 4718596
  185.9 1.3 copy-start.3
  185.9 2.0 %copy-start.4 = (f32[48,768]{1,0:T(8,128)S(1)}, f32[48,768]{1,0:T(8,128)}, u32[]{:S(2)}) copy-start(f32[48,768]{1,0:T(8,128)} %get-tuple-element.57) | copy-start | bytes 442372
  185.9 2.7 %copy-start.2 = (f32[48,3072]{1,0:T(8,128)S(1)}, f32[48,3072]{1,0:T(8,128)}, u32[]{:S(2)}) copy-start(f32[48,3072]{1,0:T(8,128)} %get-tuple-element.58) | copy-start | bytes 1769476
  187.1 2.2 %copy-start.1 = (f32[192,768]{1,0:T(8,128)S(1)}, f32[192,768]{1,0:T(8,128)}, u32[]{:S(2)}) copy-start(f32[192,768]{1,0:T(8,128)} %get-tuple-element.59) | copy-start | bytes 1769476

commit v3 on v2

--- a/solution.py
+++ b/solution.py
@@ -323,7 +323,7 @@
         return start
 
 
-BIAS_Q, BIAS_V, BIAS_OUT, BIAS_DOWN, GAIN_1, SHIFT_1, GAIN_2, SHIFT_2, BIAS_UP = range(9)
+BIAS_Q, BIAS_V, GAIN_1, SHIFT_1, BIAS_OUT, BIAS_DOWN, GAIN_2, SHIFT_2, BIAS_UP = range(9)
 TABLE = 16
 FAR_COUNT = 240
 NEAR_COUNT = 32
@@ -335,10 +335,10 @@
     wq, wo, wu, wd, gwq, gwd,
     tok, tok_far, first, first_t, qkv, k_t, v_t, lower, lse, o_t,
     mixed_near, mixed, mixed_t, middle, second, second_t, gout,
-    hidden, hidden_t, slope, gmix_head, dk, dv,
+    hidden, hidden_t, slope, pieces,
     e_own, e_z, e_y, e_c, vec, gvec, v_z, v_y, v_c, v_x, v_sum,
-    r1_d, rx_d, ry_d, rz_d, r5_d, r1_u, r2_u, r3_u, r5_u,
-    r1_o, r2_o, r3_o, r5_o, r1_q, r2_q, r3_q, r5_q,
+    r1_d, rx_d, ry_d, rz_d, r5_d, r1_u, rx_u, ry_u, rz_u, r5_u,
+    r2_u, r3_u, r4_u, r1_o, r2_o, r3_o, r4_o, r1_q, r2_q, r3_q, r5_q,
     near_sem, send_sem, recv_sem,
 ):
     d = lax.axis_index("dp")
@@ -499,17 +499,13 @@
             lambda dz: tile_lanes(turn(i, lax.rem(z + dz, zs))),
         )
 
-    cuts = local // 128 - 1
+    cuts = local // 128
     base_gd = number.take(cuts * (zs + 6))
-    base_gw = number.take(2 * steps)
 
     def gather_d(i):
         mine = pl.ds(pl.multiple_of(s * local + i * 128, 128), 128)
         others = pl.ds(pl.multiple_of((1 - s) * local + i * 128, 128), 128)
         return GatherHalf(wd, rd, mine, others, base_gd + i * (zs + 6), own_d)
-
-    def gather_w(i):
-        return Gather(wd, rd, pl.ds(i * local + cuts * 128, 128), base_gw + i * steps, own_d)
 
     near_q = []
     for p in range(pairs):
@@ -523,11 +519,14 @@
                 )
             )
     near_rest = []
-    for own, whole, r in ((own_o, wo, rq), (own_u, wu, rq), (own_d, wd, rd)):
+    half = pl.ds(pl.multiple_of(s * local, 128), local)
+    for own, there in (
+        (own_o, wo.at[z, block_rows(rq, y, c), :]),
+        (own_u, wu.at[z, block_rows(rq, y, c), :]),
+        (own_d.at[:, half], wd.at[z, block_rows(rd, y, c), half]),
+    ):
         near_rest.append(
-            pltpu.make_async_copy(
-                own, whole.at[z, block_rows(r, y, c), :], near_sem.at[local_number.take(1)]
-            )
+            pltpu.make_async_copy(own, there, near_sem.at[local_number.take(1)])
         )
     near_cot = pltpu.make_async_copy(cot, gout, near_sem.at[local_number.take(1)])
     near_tok = pltpu.make_async_copy(tok_own, tok, near_sem.at[local_number.take(1)])
@@ -571,7 +570,7 @@
     e_own[1] = total.astype(BF)
     c_table = far(e_own.at[1], e_c, base_e + zs, c_peer)
     c_table.start()
-    gather_q(1).relay(gather_u(0))
+    gather_q(1).relay(gather_d(0))
     c_table.wait_recv()
     total = total + e_c[...].astype(F32)
     for i in range(TABLE):
@@ -633,13 +632,22 @@
     def pass_on(k):
         @pl.when(k == 0)
         def _():
-            gather_u(0).relay(gather_d(0))
+            gather_o.relay(gather_d(2))
+
+        @pl.when(k == 2)
+        def _():
+            gather_d(0).relay(gather_u(0))
+            gather_d(0).push_x()
             gather_o.relay_y()
 
         @pl.when(k == 3)
         def _():
-            gather_u(1).relay(gather_d(1))
-            gather_u(0).relay_y()
+            gather_d(1).relay(gather_u(1))
+            gather_d(1).push_x()
+
+        @pl.when(k == 4)
+        def _():
+            gather_d(2).relay(gather_u(2))
 
     def attend(p):
         def head(h):
@@ -689,13 +697,12 @@
         loop(rows // side, body)
 
     gather_q(0).relay_y()
-    gather_q(2).relay(gather_u(1))
+    gather_q(2).relay(gather_d(1))
     gather_q(0).finish()
     project(0, s * rows)
     gather_q(1).relay_y()
     for copy in near_rest:
         copy.wait()
-    gather_o.relay(gather_u(2))
     gather_q(2).relay_y()
     send_tok.wait_recv()
     first_norm(tok_far, (1 - s) * rows)
@@ -712,8 +719,11 @@
         keep_mixed(p).start()
 
     loop(pairs, pair_forward)
-    gather_u(2).relay(gather_u(3))
-    gather_u(1).relay_y()
+    gather_d(0).relay_y()
+    gather_d(1).relay_y()
+    gather_d(2).push_x()
+    gather_u(0).relay(gather_u(3))
+    gather_d(2).relay_y()
 
     gather_o.finish()
     near_cot.wait()
@@ -736,21 +746,21 @@
         rounded = (scaled * vec[GAIN_2] + vec[SHIFT_2]).astype(BF)
         second[at, :] = rounded
         second_t[:, at] = rounded.T
-        gtok[at, :] = jnp.zeros((128, width), F32)
         spot = s * rows + i * 128 + lax.broadcasted_iota(jnp.int32, (128, width), 0)
         gout[at, :] = jnp.where(spot < last_valid, gout[at, :].astype(F32), 0.0).astype(BF)
 
     loop(rows // 128, project_out)
-    gather_d(0).relay(gather_w(0))
-    gather_d(0).push_x()
-
-
-    base_sib = number.take(tiles * 4)
+    for p in range(pairs):
+        send_mixed(p).wait_send()
+    gather_d(0).relay_x()
+    gather_u(1).relay()
+    gather_u(0).relay_y()
+
+
+    base_sib = number.take(tiles * 2)
     base_dx = number.take(tiles * 2)
-    base_uy = number.take(tiles)
     base_zd = number.take(zs - 1)
-    base_zu = number.take(tiles * (zs - 1))
-    base_xs = number.take(2)
+    base_xs = number.take(1)
     mine = pl.ds(pl.multiple_of(s * local, 128), local)
     others = pl.ds(pl.multiple_of((1 - s) * local, 128), local)
 
@@ -760,7 +770,7 @@
     def sib_d(t, yy):
         return far_g(
             gwd.at[t, block_rows(rd, yy, 1 - c), :], r1_d.at[t, rows_y(rd, yy), :],
-            base_sib + t * 4 + yy, c_peer,
+            base_sib + t * 2 + yy, c_peer,
         )
 
     def sib_start_d(t):
@@ -799,161 +809,265 @@
         def _():
             z_d(t, dz).start()
 
-    def sib_u(t, yy):
-        return far_g(
-            wu.at[:, block_rows(rq, yy, 1 - c), tile_lanes(t)],
-            r1_u.at[:, rows_y(rq, yy), tile_lanes(t)],
-            base_sib + t * 4 + 2 + yy, c_peer,
+    class Pooled:
+        def __init__(self, ref, start, span, parts, base):
+            self.ref, self.base = ref, base
+            self.r1, self.rx, self.ry, self.rz, self.r5 = parts
+            half = span // 2
+            self.full = pl.ds(pl.multiple_of(start, 128), span)
+            self.mine = pl.ds(pl.multiple_of(start + s * half, 128), half)
+            self.others = pl.ds(pl.multiple_of(start + (1 - s) * half, 128), half)
+            self.narrow = pl.ds(pl.multiple_of((start - early * span) // 2, 128), half)
+
+        def sib(self, yy):
+            return far_g(
+                self.ref.at[:, block_rows(rq, yy, 1 - c), self.full],
+                self.r1.at[:, rows_y(rq, yy), self.full], self.base + yy, c_peer,
+            )
+
+        def sib_start(self):
+            for yy in range(2):
+                self.sib(yy).start()
+
+        def along_x(self):
+            return far_g(
+                self.r1.at[:, :, self.others], self.rx.at[:, :, self.narrow], self.base + 2, x_peer
+            )
+
+        def x_start(self):
+            for yy in range(2):
+                self.sib(yy).wait_recv()
+                at = rows_y(rq, yy)
+                for zz in range(zs):
+                    self.r1[zz, at, self.full] = (
+                        self.r1[zz, at, self.full].astype(F32)
+                        + self.ref[zz, block_rows(rq, yy, c), self.full].astype(F32)
+                    ).astype(BF)
+            self.along_x().start()
+
+        def along_y(self):
+            return far_g(
+                self.rx.at[:, rows_y(rq, 1 - y), self.narrow], self.ry.at[:, :, self.narrow],
+                self.base + 3, y_peer,
+            )
+
+        def y_start(self):
+            self.along_x().wait_recv()
+            for zz in range(zs):
+                self.rx[zz, :, self.narrow] = (
+                    self.rx[zz, :, self.narrow].astype(F32)
+                    + self.r1[zz, :, self.mine].astype(F32)
+                ).astype(BF)
+            self.along_y().start()
+
+        def along_z(self, dz):
+            return far_g(
+                self.ry.at[lax.rem(z + dz, zs), :, self.narrow],
+                self.rz.at[dz - 1, :, self.narrow], self.base + 3 + dz, z_peers[dz - 1],
+            )
+
+        def z_start(self):
+            self.along_y().wait_recv()
+            at = rows_y(rq, y)
+            for zz in range(zs):
+                self.ry[zz, :, self.narrow] = (
+                    self.ry[zz, :, self.narrow].astype(F32)
+                    + self.rx[zz, at, self.narrow].astype(F32)
+                ).astype(BF)
+            for dz in range(1, zs):
+                self.along_z(dz).start()
+
+        def swap(self, half):
+            block = self.r5.at[half, :, self.narrow]
+            return far_g(block, block, self.base + 3 + zs, x_peer)
+
+        def finish(self):
+            total = self.ry[z, :, self.narrow].astype(F32)
+            for dz in range(1, zs):
+                self.along_z(dz).wait_recv()
+                total = total + self.rz[dz - 1, :, self.narrow].astype(F32)
+            self.r5[s, :, self.narrow] = total.astype(BF)
+            self.swap(s).start()
+
+        def sent(self):
+            for yy in range(2):
+                self.sib(yy).wait_send()
+            self.along_x().wait_send()
+            self.along_y().wait_send()
+            for dz in range(1, zs):
+                self.along_z(dz).wait_send()
+            self.swap(s).wait_send()
+
+    class Spread:
+        def __init__(self, ref, columns, r1, r2, r3, base):
+            self.ref, self.columns, self.r1, self.r2, self.r3 = ref, columns, r1, r2, r3
+            self.base = base
+
+        def sib(self, yy):
+            return far_g(
+                self.ref.at[:, block_rows(rq, yy, 1 - c), self.columns],
+                self.r1.at[:, pl.ds(pl.multiple_of(yy * rq, rq), rq), self.columns],
+                self.base + yy, c_peer,
+            )
+
+        def sib_start(self):
+            self.sib(1 - y).start()
+            self.sib(y).start()
+
+        def along_y(self):
+            return far_g(
+                self.r1.at[:, pl.ds(pl.multiple_of((1 - y) * rq, rq), rq), self.columns],
+                self.r2.at[:, :, self.columns], self.base + 2, y_peer,
+            )
+
+        def y_start(self):
+            self.sib(1 - y).wait_recv()
+            at = pl.ds(pl.multiple_of((1 - y) * rq, rq), rq)
+            for zz in range(zs):
+                self.r1[zz, at, self.columns] = (
+                    self.r1[zz, at, self.columns].astype(F32)
+                    + self.ref[zz, block_rows(rq, 1 - y, c), self.columns].astype(F32)
+                ).astype(BF)
+            self.along_y().start()
+
+        def along_z(self, dz):
+            return far_g(
+                self.r2.at[lax.rem(z + dz, zs), :, self.columns],
+                self.r3.at[dz - 1, :, self.columns], self.base + 2 + dz, z_peers[dz - 1],
+            )
+
+        def z_start(self):
+            self.sib(y).wait_recv()
+            self.along_y().wait_recv()
+            at = pl.ds(pl.multiple_of(y * rq, rq), rq)
+            for zz in range(zs):
+                self.r2[zz, :, self.columns] = (
+                    self.r2[zz, :, self.columns].astype(F32)
+                    + self.r1[zz, at, self.columns].astype(F32)
+                    + self.ref[zz, block_rows(rq, y, c), self.columns].astype(F32)
+                ).astype(BF)
+            for dz in range(1, zs):
+                self.along_z(dz).start()
+
+        def z_finish(self):
+            total = self.r2[z, :, self.columns].astype(F32)
+            for dz in range(1, zs):
+                self.along_z(dz).wait_recv()
+                total = total + self.r3[dz - 1, :, self.columns].astype(F32)
+            return total
+
+        def sent(self):
+            self.sib(0).wait_send()
+            self.sib(1).wait_send()
+            self.along_y().wait_send()
+            for dz in range(1, zs):
+                self.along_z(dz).wait_send()
+
+    def swap(parts, columns, slot):
+        return far_g(parts.at[0, :, columns], parts.at[1, :, columns], slot, x_peer)
+
+    early = tiles // 2
+    spread_steps = zs + 2
+    base_su = number.take(early * (spread_steps + 1))
+
+    def sum_e(t):
+        return Spread(
+            wu, tile_lanes(t), r1_u, r2_u, r3_u, base_su + t * (spread_steps + 1)
         )
 
-    def sib_start_u(t):
-        for yy in (1 - y, y):
-            sib_u(t, yy).start()
-
-    def y_u(t):
-        return far_g(
-            r1_u.at[:, rows_y(rq, 1 - y), tile_lanes(t)], r2_u.at[:, :, tile_lanes(t)],
-            base_uy + t, y_peer,
-        )
-
-    def y_start_u(t):
-        yy = 1 - y
-        sib_u(t, yy).wait_recv()
-        at = rows_y(rq, yy)
-        for zz in range(zs):
-            r1_u[zz, at, tile_lanes(t)] = (
-                r1_u[zz, at, tile_lanes(t)].astype(F32)
-                + wu[zz, block_rows(rq, yy, c), tile_lanes(t)].astype(F32)
-            ).astype(BF)
-        y_u(t).start()
-
-    def z_u(t, dz):
-        return far_g(
-            r2_u.at[lax.rem(z + dz, zs), :, tile_lanes(t)], r3_u.at[dz - 1, :, tile_lanes(t)],
-            base_zu + t * (zs - 1) + dz - 1, z_peers[dz - 1],
-        )
-
-    def z_start_u(t):
-        sib_u(t, y).wait_recv()
-        y_u(t).wait_recv()
-        at = rows_y(rq, y)
-        for zz in range(zs):
-            r2_u[zz, :, tile_lanes(t)] = (
-                r2_u[zz, :, tile_lanes(t)].astype(F32)
-                + r1_u[zz, at, tile_lanes(t)].astype(F32)
-                + wu[zz, block_rows(rq, y, c), tile_lanes(t)].astype(F32)
-            ).astype(BF)
-        for step in range(1, zs):
-            z_u(t, step).start()
-
-    sub = 256
+    def swap_e(t):
+        return swap(r4_u, tile_lanes(t), base_su + t * (spread_steps + 1) + spread_steps)
+
+    def finish_e(t):
+        r4_u[0, :, tile_lanes(t)] = sum_e(t).z_finish().astype(BF)
+        swap_e(t).start()
+
+    whole = pl.ds(0, width)
+    sum_o = Spread(wo, whole, r1_o, r2_o, r3_o, number.take(spread_steps))
+    swap_o = swap(r4_o, whole, number.take(1))
+
+    def finish_o():
+        r4_o[0] = sum_o.z_finish().astype(BF)
+        swap_o.start()
+
+    pooled_steps = zs + 4
+    base_pu = number.take(tiles * pooled_steps)
+
+    def sum_u(t):
+        return Pooled(wu, t * tile, tile, (r1_u, rx_u, ry_u, rz_u, r5_u), base_pu + t * pooled_steps)
 
     def pass_up(k):
+        @pl.when(k == 0)
+        def _():
+            gather_d(1).relay_x()
+
         @pl.when(k == 1)
         def _():
+            gather_u(2).relay()
+            gather_u(1).relay_y()
+
+        @pl.when(k == 2)
+        def _():
+            x_start_d(turn(0, z))
+
+        @pl.when(k == 3)
+        def _():
+            gather_u(3).relay()
             gather_u(2).relay_y()
 
-        @pl.when(k == 2)
-        def _():
-            gather_d(1).relay(gather_w(1))
-            gather_d(1).push_x()
-
-        @pl.when(k == 3)
-        def _():
-            gather_d(0).relay_y()
-
         @pl.when(k == 4)
         def _():
-            x_start_d(turn(0, z))
+            gather_d(2).relay_x()
+            x_start_d(turn(1, z))
 
         @pl.when(k == 5)
         def _():
-            gather_u(3).relay()
+            gather_u(3).relay_y()
 
         @pl.when(k == 6)
         def _():
-            gather_d(1).relay_y()
-            gather_d(0).relay_x()
-
-        @pl.when(k == 7)
-        def _():
-            gather_w(0).relay()
-
-        @pl.when(k == 8)
-        def _():
-            gather_u(3).relay_y()
-
-        @pl.when(k == 9)
-        def _():
-            gather_w(1).relay()
-            gather_d(1).relay_x()
-
-        @pl.when(k == 10)
-        def _():
-            gather_w(0).relay_y()
-            x_start_d(turn(1, z))
+            x_start_d(turn(2, z))
 
     def feed(i):
         t = turn(i, z)
         gather_u(i).finish()
-
-        def part(u):
-            at = pl.ds(pl.multiple_of(t * tile + u * sub, 128), sub)
-            near = pl.ds(pl.multiple_of(u * sub, sub), sub)
-            pre = mul(second[...], flat(wu[:, :, at])) + vec[BIAS_UP + t, :, near]
-            bent = jnp.tanh(SLOPE * (pre + CUBIC * pre * pre * pre))
-            value = (0.5 * pre * (1.0 + bent)).astype(BF)
-            bend = 0.5 * (1.0 + bent) + 0.5 * pre * (1.0 - bent * bent) * SLOPE * (
-                1.0 + 3.0 * CUBIC * pre * pre
-            )
-            hidden[:, at] = value
-            hidden_t[near, :] = value.T
-            slope[:, at] = bend.astype(BF)
-            pass_up(i * (tile // sub) + u)
-
-        loop(tile // sub, part)
-
-        def weigh(m):
-            at = pl.ds(pl.multiple_of(m * rd, rd), rd)
-            gwd[t, at, :] = mul(hidden_t[at, :], gout[...]).astype(BF)
-
-        loop(4, weigh)
+        at = tile_lanes(t)
+        pre = mul(second[...], flat(wu[:, :, at])) + vec[BIAS_UP + t]
+        square = pre * pre
+        bent = 0.5 * jnp.tanh(pre * (SLOPE + (SLOPE * CUBIC) * square)) + 0.5
+        value = pre * bent
+        bend = bent + value * (1.0 - bent) * (2.0 * SLOPE + (6.0 * SLOPE * CUBIC) * square)
+        rounded = value.astype(BF)
+        hidden[:, at] = rounded
+        hidden_t[...] = rounded.T
+        slope[:, at] = bend.astype(BF)
+        pass_up(i * 2)
+        gwd[t] = mul(hidden_t[...], gout[...]).astype(BF)
         sib_start_d(t)
+        pass_up(i * 2 + 1)
 
     loop(tiles, feed)
     y_start_d(turn(0, z))
-    x_start_d(turn(2, z))
-    gather_w(1).relay_y()
     for i in range(cuts):
         gather_d(i).finish()
-    for i in range(2):
-        gather_w(i).finish()
-
-    def slopes_back(i):
-        at = pl.ds(pl.multiple_of(i * sub, sub), sub)
-        t = lax.div(i, tile // sub)
-        near = pl.ds(pl.multiple_of((i - t * (tile // sub)) * sub, sub), sub)
-        grad = (mul_nt(gout[...], wd[t, near, :]) * slope[:, at].astype(F32)).astype(BF)
+
+    def slopes_back(t):
+        at = tile_lanes(t)
+        grad = (mul_nt(gout[...], wd[t]) * slope[:, at].astype(F32)).astype(BF)
         slope[:, at] = grad
-        gvec[BIAS_UP + t, :, near] = column_sum(grad.astype(F32))
-
-    loop(tiles * (tile // sub), slopes_back)
+        gvec[BIAS_UP + t] = column_sum(grad.astype(F32))
+
+    loop(tiles, slopes_back)
     y_start_d(turn(1, z))
-    x_start_d(z)
     z_start_d(turn(0, z))
 
-    def grow(t):
-        def add(i):
-            at = pl.ds(pl.multiple_of(i * side, side), side)
-            gtok[at, :] += mul_nt(slope[at, tile_lanes(t)], flat(wu[:, :, tile_lanes(t)]))
-
-        loop(rows // side, add)
-
-    loop(tiles, grow)
+    def grow(i):
+        at = pl.ds(pl.multiple_of(i * side, side), side)
+        gtok[at, :] = mul_nt(slope[at, :], flat(wu[...]))
+
+    loop(rows // side, grow)
 
     for row in (BIAS_Q, BIAS_V, BIAS_OUT, BIAS_DOWN, GAIN_1, SHIFT_1, GAIN_2, SHIFT_2):
-        gvec[row] = jnp.zeros((1, width), F32)
-    for row in range(BIAS_UP + tiles, TABLE):
         gvec[row] = jnp.zeros((1, width), F32)
     gattn = mixed
     gmix = second
@@ -975,6 +1089,54 @@
 
     loop(rows // 128, middle_back)
 
+    class Vectors:
+        def __init__(self, first_row, count, base):
+            self.rows, self.base = range(first_row, first_row + count), base
+            self.at = pl.ds(first_row, count)
+
+        def copy(self, source, there, slot, device):
+            return far(source.at[self.at], there.at[self.at], self.base + slot, device)
+
+        def along_z(self, dz):
+            return self.copy(gvec, v_z.at[dz - 1], dz - 1, z_peers[dz - 1])
+
+        def step(self, k):
+            there, device = ((v_y, y_peer), (v_c, c_peer), (v_x, x_peer))[k]
+            return self.copy(v_sum.at[k], there, zs - 1 + k, device)
+
+        def z_start(self):
+            for dz in range(1, zs):
+                self.along_z(dz).start()
+
+        def y_start(self):
+            for dz in range(1, zs):
+                self.along_z(dz).wait_recv()
+            for i in self.rows:
+                total = gvec[i]
+                for dz in range(1, zs):
+                    total = total + v_z[dz - 1, i]
+                v_sum[0, i] = total
+            self.step(0).start()
+
+        def next_start(self, k):
+            self.step(k - 1).wait_recv()
+            there = (v_y, v_c)[k - 1]
+            v_sum[k, self.at] = v_sum[k - 1, self.at] + there[self.at]
+            self.step(k).start()
+
+        def finish(self):
+            self.step(2).wait_recv()
+            out_v[self.at] = v_sum[2, self.at] + v_x[self.at]
+
+        def sent(self):
+            for dz in range(1, zs):
+                self.along_z(dz).wait_send()
+            for k in range(3):
+                self.step(k).wait_send()
+
+    late_rows = Vectors(BIAS_Q, 4, number.take(zs + 2))
+    early_rows = Vectors(BIAS_OUT, 4 + tiles, number.take(zs + 2))
+
     base_gmix = number.take(pairs)
     near_gmix = local_number.take(1)
     here_rows = pl.ds(pl.multiple_of(s * rows, 128), rows)
@@ -983,98 +1145,30 @@
     def send_gmix(p):
         lanes_p = pl.ds(pl.multiple_of((1 - s) * local + p * 128, 128), 128)
         at = pl.ds(pl.multiple_of(p * 128, 128), 128)
-        return far(gmix.at[:, lanes_p], gmix_head.at[here_rows, at], base_gmix + p, x_peer)
+        return far(gmix.at[:, lanes_p], mixed_near.at[here_rows, at], base_gmix + p, x_peer)
 
     def take_gmix(p):
         at = pl.ds(pl.multiple_of(p * 128, 128), 128)
-        return far(gmix.at[:, pl.ds(0, 128)], gmix_head.at[there_rows, at], base_gmix + p, x_peer)
+        return far(gmix.at[:, pl.ds(0, 128)], mixed_near.at[there_rows, at], base_gmix + p, x_peer)
 
     keep_gmix = pltpu.make_async_copy(
-        gmix.at[:, mine], gmix_head.at[here_rows, :], near_sem.at[near_gmix]
-    )
-    for p in range(pairs):
+        gmix.at[:, mine], mixed_near.at[here_rows, :], near_sem.at[near_gmix]
+    )
+    send_gmix(0).start()
+    keep_gmix.start()
+    x_start_d(z)
+    for p in range(1, pairs):
         send_gmix(p).start()
-    keep_gmix.start()
+    early_rows.z_start()
 
     gather_o.sent()
 
-    def weigh_out(m):
-        at = pl.ds(pl.multiple_of(m * 4 * rq, 4 * rq), 4 * rq)
-        wo[m] = mul(mixed_t[at, :], gattn[...]).astype(BF)
-
-    loop(zs, weigh_out)
+    wo[...] = mul(mixed_t[...], gattn[...]).astype(BF).reshape(zs, 4 * rq, width)
     y_start_d(turn(2, z))
     z_start_d(turn(1, z))
     for t in range(tiles):
         gather_u(t).sent()
 
-    class Spread:
-        def __init__(self, ref, columns, r1, r2, r3, base):
-            self.ref, self.columns, self.r1, self.r2, self.r3 = ref, columns, r1, r2, r3
-            self.base = base
-
-        def sib(self, yy):
-            return far_g(
-                self.ref.at[:, block_rows(rq, yy, 1 - c), self.columns],
-                self.r1.at[:, pl.ds(pl.multiple_of(yy * rq, rq), rq), self.columns],
-                self.base + yy, c_peer,
-            )
-
-        def sib_start(self):
-            self.sib(1 - y).start()
-            self.sib(y).start()
-
-        def along_y(self):
-            return far_g(
-                self.r1.at[:, pl.ds(pl.multiple_of((1 - y) * rq, rq), rq), self.columns],
-                self.r2.at[:, :, self.columns], self.base + 2, y_peer,
-            )
-
-        def y_start(self):
-            self.sib(1 - y).wait_recv()
-            at = pl.ds(pl.multiple_of((1 - y) * rq, rq), rq)
-            for zz in range(zs):
-                self.r1[zz, at, self.columns] = (
-                    self.r1[zz, at, self.columns].astype(F32)
-                    + self.ref[zz, block_rows(rq, 1 - y, c), self.columns].astype(F32)
-                ).astype(BF)
-            self.along_y().start()
-
-        def along_z(self, dz):
-            return far_g(
-                self.r2.at[lax.rem(z + dz, zs), :, self.columns],
-                self.r3.at[dz - 1, :, self.columns], self.base + 2 + dz, z_peers[dz - 1],
-            )
-
-        def z_start(self):
-            self.sib(y).wait_recv()
-            self.along_y().wait_recv()
-            at = pl.ds(pl.multiple_of(y * rq, rq), rq)
-            for zz in range(zs):
-                self.r2[zz, :, self.columns] = (
-                    self.r2[zz, :, self.columns].astype(F32)
-                    + self.r1[zz, at, self.columns].astype(F32)
-                    + self.ref[zz, block_rows(rq, y, c), self.columns].astype(F32)
-                ).astype(BF)
-            for dz in range(1, zs):
-                self.along_z(dz).start()
-
-        def z_finish(self):
-            total = self.r2[z, :, self.columns].astype(F32)
-            for dz in range(1, zs):
-                self.along_z(dz).wait_recv()
-                total = total + self.r3[dz - 1, :, self.columns].astype(F32)
-            return total
-
-        def sent(self):
-            self.sib(0).wait_send()
-            self.sib(1).wait_send()
-            self.along_y().wait_send()
-            for dz in range(1, zs):
-                self.along_z(dz).wait_send()
-
-    spread_steps = zs + 2
-    sum_o = Spread(wo, pl.ds(0, width), r1_o, r2_o, r3_o, number.take(spread_steps))
     base_sq = number.take(pairs * spread_steps)
 
     def sum_q(p):
@@ -1086,49 +1180,38 @@
     sum_o.sib_start()
 
     def weigh_up_tile(t):
-        def weigh_up(m):
-            at = pl.ds(pl.multiple_of(m * 4 * rq, 4 * rq), 4 * rq)
-            wu[m, :, tile_lanes(t)] = mul(second_t[at, :], slope[:, tile_lanes(t)]).astype(BF)
-
-        loop(zs, weigh_up)
-        sib_start_u(t)
+        at = tile_lanes(t)
+        wu[:, :, at] = mul(second_t[...], slope[:, at]).astype(BF).reshape(zs, 4 * rq, tile)
+        @pl.when(t < early)
+        def _():
+            sum_e(t).sib_start()
+
+        @pl.when(t >= early)
+        def _():
+            sum_u(t).sib_start()
 
         @pl.when(t == 0)
         def _():
             sum_o.y_start()
 
-        @pl.when(t > 0)
-        def _():
-            y_start_u(t - 1)
-
-        @pl.when(t == 2)
-        def _():
-            y_start_d(z)
-            z_start_d(turn(2, z))
+        @pl.when(t == 1)
+        def _():
+            early_rows.y_start()
+
+        @pl.when((t > 0) & (t <= early))
+        def _():
+            sum_e(t - 1).y_start()
+
+        @pl.when(t > early)
+        def _():
+            sum_u(t - 1).x_start()
 
     loop(tiles, weigh_up_tile)
-    y_start_u(tiles - 1)
-
-    def fall(t):
-        def add(i):
-            at = pl.ds(pl.multiple_of(i * side, side), side)
-            middle[at, :] += mul(hidden[at, tile_lanes(t)], wd[t])
-
-        loop(rows // side, add)
-
-    loop(tiles, fall)
-
-    def finish_out(i):
-        at = pl.ds(pl.multiple_of(i * 128, 128), 128)
-        value = middle[at, :] + vec[BIAS_DOWN]
-        spot = s * rows + i * 128 + lax.broadcasted_iota(jnp.int32, (128, width), 0)
-        out[at, :] = jnp.where(spot < last_valid, value, 0.0).astype(BF)
-
-    loop(rows // 128, finish_out)
+    z_start_d(turn(2, z))
+    sum_u(tiles - 1).x_start()
     keep_gmix.wait()
 
     xd = far_g(r5_d.at[s], r5_d.at[s], base_xs, x_peer)
-    xo = far_g(r5_o.at[0], r5_o.at[1], number.take(1), x_peer)
 
     def finish_d():
         total = ry_d[z].astype(F32)
@@ -1138,35 +1221,50 @@
         r5_d[s] = total.astype(BF)
         xd.start()
 
-    def finish_o():
-        r5_o[0] = sum_o.z_finish().astype(BF)
-        xo.start()
-
     def serve(k):
         @pl.when(k == 0)
         def _():
+            early_rows.next_start(1)
             sum_o.z_start()
+            y_start_d(z)
+
+        @pl.when(k == 1)
+        def _():
+            early_rows.next_start(2)
 
         @pl.when(k == 2)
         def _():
-            z_start_u(0)
+            sum_e(0).z_start()
+            sum_q(0).y_start()
 
         @pl.when(k == 3)
         def _():
-            z_start_u(1)
+            sum_e(1).z_start()
             finish_o()
 
         @pl.when(k == 4)
         def _():
-            z_start_u(2)
+            sum_u(2).y_start()
+            sum_q(1).y_start()
+            z_start_d(z)
 
         @pl.when(k == 5)
         def _():
-            z_start_d(z)
+            sum_u(3).y_start()
+            sum_q(0).z_start()
+            finish_e(0)
+
+    per_piece = rows // side
+
+    def dk_at(j):
+        return (j // per_piece, slice(j % per_piece * side, (j % per_piece + 1) * side))
+
+    def dv_at(j):
+        return dk_at(j + blocks)
 
     def attend_back(p):
-        dk[...] = jnp.zeros_like(dk)
-        dv[...] = jnp.zeros_like(dv)
+        for i in range(2 * group // rows):
+            pieces[i] = jnp.zeros((rows, 128), F32)
 
         def head(h):
             half = pl.ds(pl.multiple_of(h * HEAD_DIM, HEAD_DIM), HEAD_DIM)
@@ -1174,7 +1272,7 @@
             for qi in range(blocks):
                 at = slice(qi * side, (qi + 1) * side)
                 query = head_lanes(qkv[at, lanes(p, 0)].astype(F32) * scale, h)
-                grad = head_lanes(gmix_head[at, here].astype(F32), h)
+                grad = head_lanes(mixed_near[at, here].astype(F32), h)
                 level = lse[p, h, :, at]
                 weights, slopes = [], []
                 centre = jnp.zeros((1, side), F32)
@@ -1190,8 +1288,8 @@
                 for j in range(qi + 1):
                     there = slice(j * side, (j + 1) * side)
                     bend = (weights[j] * (slopes[j] - centre)).astype(BF)
-                    dk[there, :] += mul(bend, query)
-                    dv[there, :] += mul(weights[j].astype(BF), grad)
+                    pieces[dk_at(j)] += mul(bend, query)
+                    pieces[dv_at(j)] += mul(weights[j].astype(BF), grad)
                     total = total + mul(k_t[p, half, there], bend)
                 o_t[half, at] = total * scale
             serve(p * 2 + h)
@@ -1200,27 +1298,19 @@
         for qi in range(blocks):
             at = slice(qi * side, (qi + 1) * side)
             qkv[at, lanes(p, 0)] = o_t[:, at].T.astype(BF)
-            qkv[at, lanes(p, 1)] = dk[at, :].astype(BF)
-            qkv[at, lanes(p, 2)] = dv[at, :].astype(BF)
+            qkv[at, lanes(p, 1)] = pieces[dk_at(qi)].astype(BF)
+            qkv[at, lanes(p, 2)] = pieces[dv_at(qi)].astype(BF)
         own = pl.ds(pl.multiple_of(s * local + p * 128, 128), 128)
         gvec[BIAS_Q, :, own] = column_sum(qkv[:, lanes(p, 0)].astype(F32))
         gvec[BIAS_V, :, own] = column_sum(qkv[:, lanes(p, 2)].astype(F32))
         both = pl.ds(pl.multiple_of(p * local, 128), local)
 
-        def weigh(m):
-            at = pl.ds(pl.multiple_of(m * 4 * rq, 4 * rq), 4 * rq)
-            gwq[m, :, both] = mul(first_t[at, :], qkv[:, both]).astype(BF)
-
-        loop(zs, weigh)
+        gwq[:, :, both] = mul(first_t[...], qkv[:, both]).astype(BF).reshape(zs, 4 * rq, local)
 
     def pair_back(p):
         take_gmix(p).wait_recv()
         attend_back(p)
         sum_q(p).sib_start()
-
-        @pl.when(p > 0)
-        def _():
-            sum_q(p - 1).y_start()
 
     loop(pairs, pair_back)
 
@@ -1245,83 +1335,93 @@
         send_gf(i).start()
 
     loop(rows // side, away)
-    sum_q(pairs - 1).y_start()
-    z_start_u(3)
+    sum_q(2).y_start()
 
     def stay(i):
-        middle[pl.ds(pl.multiple_of(i * side, side), side), :] = first_back(i, tok, s * rows)
+        grad = first_back(i, tok, s * rows)
+        at = pl.ds(pl.multiple_of(i * side, side), side)
+        for j in range(width // 128):
+            pieces[j, at, :] = grad[:, j * 128 : (j + 1) * 128]
 
     loop(rows // side, stay)
 
-    base_v = number.take(zs + 2)
-    for dz in range(1, zs):
-        far(gvec, v_z.at[dz - 1], base_v + dz - 1, z_peers[dz - 1]).start()
-    for dz in range(1, zs):
-        far(gvec, v_z.at[dz - 1], base_v + dz - 1, z_peers[dz - 1]).wait_recv()
-    for i in range(TABLE):
-        total = gvec[i]
-        for dz in range(1, zs):
-            total = total + v_z[dz - 1, i]
-        v_sum[0, i] = total
-    vy = far(v_sum.at[0], v_y, base_v + zs - 1, y_peer)
-    vy.start()
-    for p in range(pairs):
-        sum_q(p).z_start()
-    vy.wait_recv()
-    v_sum[1] = v_sum[0] + v_y[...]
-    vc = far(v_sum.at[1], v_c, base_v + zs, c_peer)
-    vc.start()
-    vc.wait_recv()
-    v_sum[2] = v_sum[1] + v_c[...]
-    vx = far(v_sum.at[2], v_x, base_v + zs + 1, x_peer)
-    vx.start()
-
+    late_rows.z_start()
+    sum_u(2).z_start()
+    sum_q(1).z_start()
     finish_d()
-    for t in range(tiles):
-        for dz in range(1, zs):
-            z_u(t, dz).wait_recv()
-
-    def finish_u(t):
-        total = r2_u[z, :, tile_lanes(t)].astype(F32)
-        for dz in range(1, zs):
-            total = total + r3_u[dz - 1, :, tile_lanes(t)].astype(F32)
-        r5_u[0, :, tile_lanes(t)] = total.astype(BF)
-
-    loop(tiles, finish_u)
-    xu = far_g(r5_u.at[0], r5_u.at[1], base_xs + 1, x_peer)
-    xu.start()
-    for p in range(pairs):
+    sum_u(3).z_start()
+
+    def fall(i):
+        at = pl.ds(pl.multiple_of(i * side, side), side)
+        middle[at, :] += mul(hidden[at, :], flat(wd[...]))
+
+    loop(rows // side, fall)
+    late_rows.y_start()
+    sum_q(2).z_start()
+
+    def finish_out(i):
+        at = pl.ds(pl.multiple_of(i * 128, 128), 128)
+        value = middle[at, :] + vec[BIAS_DOWN]
+        spot = s * rows + i * 128 + lax.broadcasted_iota(jnp.int32, (128, width), 0)
+        out[at, :] = jnp.where(spot < last_valid, value, 0.0).astype(BF)
+
+    loop(rows // 128, finish_out)
+    finish_e(1)
+    sum_u(2).finish()
+
+    slot_q = number.take(pairs)
+
+    def swap_q(p, half):
+        block = r5_q.at[half, :, pl.ds(p * local, local)]
+        return far_g(block, block, slot_q + p, x_peer)
+
+    def finish_q(p):
         r5_q[s, :, p * local : (p + 1) * local] = sum_q(p).z_finish().astype(BF)
-    slot_q = number.take(1)
-    xq = far_g(r5_q.at[s], r5_q.at[s], slot_q, x_peer)
-    xq.start()
-
-    for i in range(rows // side):
+        swap_q(p, s).start()
+
+    finish_q(0)
+    late_rows.next_start(1)
+    finish_q(1)
+    late_rows.next_start(2)
+    sum_u(3).finish()
+
+    def last(i):
+        at = pl.ds(pl.multiple_of(i * side, side), side)
         send_gf(i).wait_recv()
-
-    def last(i):
-        at = pl.ds(pl.multiple_of(i * 128, 128), 128)
         scaled, inverse = normed(tok[at, :].astype(F32))
-        there = pl.ds(pl.multiple_of(rows + i * 128, 128), 128)
-        grad = middle[at, :] + first[there, :].astype(F32)
+        there = pl.ds(pl.multiple_of(rows + i * side, side), side)
+        own = jnp.concatenate([pieces[j, at, :] for j in range(width // 128)], axis=1)
+        grad = own + first[there, :].astype(F32)
         gtok[at, :] = gtok[at, :] + normed_back(grad, scaled, inverse, vec[GAIN_1])
 
-    loop(rows // 128, last)
-
-    vx.wait_recv()
-    out_v[...] = v_sum[2] + v_x[...]
+        @pl.when(i == 0)
+        def _():
+            finish_q(2)
+
+    loop(rows // side, last)
+
+    late_rows.finish()
+    early_rows.finish()
+    for i in range(BIAS_UP + tiles, TABLE):
+        out_v[i] = jnp.zeros((1, width), F32)
     far_g(r5_d.at[1 - s], r5_d.at[1 - s], base_xs, x_peer).wait_recv()
     for half in range(2):
         out_d[:, half * local : (half + 1) * local] = r5_d[half].astype(F32)
-    xu.wait_recv()
-
-    def store_u(t):
-        out_u[:, tile_lanes(t)] = r5_u[0, :, tile_lanes(t)].astype(F32) + r5_u[1, :, tile_lanes(t)].astype(F32)
-
-    loop(tiles, store_u)
-    xo.wait_recv()
-    out_o[...] = r5_o[0].astype(F32) + r5_o[1].astype(F32)
-    far_g(r5_q.at[1 - s], r5_q.at[1 - s], slot_q, x_peer).wait_recv()
+    for t in range(early):
+        swap_e(t).wait_recv()
+        at = slice(t * tile, (t + 1) * tile)
+        out_u[:, at] = r4_u[0, :, at].astype(F32) + r4_u[1, :, at].astype(F32)
+    for t in range(early, tiles):
+        sum_u(t).swap(1 - s).wait_recv()
+        for half in range(2):
+            wide = t * tile + half * local
+            out_u[:, wide : wide + local] = r5_u[
+                half, :, (t - early) * local : (t - early + 1) * local
+            ].astype(F32)
+    swap_o.wait_recv()
+    out_o[...] = r4_o[0].astype(F32) + r4_o[1].astype(F32)
+    for p in range(pairs):
+        swap_q(p, 1 - s).wait_recv()
     for half in range(2):
         for p in range(pairs):
             for part in range(3):
@@ -1332,30 +1432,31 @@
 
     for dz in range(1, zs):
         far(table, e_z.at[dz - 1], base_e + dz - 1, z_peers[dz - 1]).wait_send()
-        far(gvec, v_z.at[dz - 1], base_v + dz - 1, z_peers[dz - 1]).wait_send()
         far_g(ry_d.at[0], rz_d.at[dz - 1], base_zd + dz - 1, z_peers[dz - 1]).wait_send()
-    for copy in (y_table, c_table, send_tok, vy, vc, vx, xd, xu, xo, xq):
+    late_rows.sent()
+    early_rows.sent()
+    for copy in (y_table, c_table, send_tok, xd):
         copy.wait_send()
     for p in range(pairs):
         gather_q(p).sent()
-        send_mixed(p).wait_send()
         sum_q(p).sent()
+        swap_q(p, s).wait_send()
     sum_o.sent()
     for i in range(cuts):
         gather_d(i).sent()
-    for i in range(2):
-        gather_w(i).sent()
     for p in range(pairs):
         send_gmix(p).wait_send()
     for t in range(tiles):
         for yy in range(2):
             sib_d(t, yy).wait_send()
-            sib_u(t, yy).wait_send()
         x_d(t).wait_send()
         y_d(t).wait_send()
-        y_u(t).wait_send()
-        for dz in range(1, zs):
-            z_u(t, dz).wait_send()
+    for t in range(early):
+        sum_e(t).sent()
+        swap_e(t).wait_send()
+    for t in range(early, tiles):
+        sum_u(t).sent()
+    swap_o.wait_send()
     for i in range(rows // side):
         send_gf(i).wait_send()
 
@@ -1401,14 +1502,16 @@
         vm((group, local)), vm((rows, width)), vm((width, rows)), vm((rows, width), F32),
         vm((rows, width)), vm((width, rows)), vm((rows, width)),
         vm((rows, deep)), vm((4 * rd, rows)), vm((rows, deep)),
-        vm((group, local)), vm((group, 128), F32), vm((group, 128), F32),
+        vm((width // 128, rows, 128), F32),
         vm((2, TABLE, width)), vm((zs - 1, TABLE, width)), vm((TABLE, width)), vm((TABLE, width)),
         vm((TABLE, 1, width), F32), vm((TABLE, 1, width), F32), vm((zs - 1, TABLE, 1, width), F32),
         vm((TABLE, 1, width), F32), vm((TABLE, 1, width), F32), vm((TABLE, 1, width), F32),
         vm((3, TABLE, 1, width), F32),
         vm((zs, 2 * rd, width)), vm((zs, 2 * rd, local)), vm((zs, rd, local)),
         vm((zs - 1, rd, local)), vm((2, rd, local)),
-        vm((zs, 2 * rq, deep)), vm((zs, rq, deep)), vm((zs - 1, rq, deep)), vm((2, rq, deep)),
+        vm((zs, 2 * rq, deep)), vm((zs, 2 * rq, deep // 4)), vm((zs, rq, deep // 4)),
+        vm((zs - 1, rq, deep // 4)), vm((2, rq, deep // 4)),
+        vm((zs, rq, deep // 2)), vm((zs - 1, rq, deep // 2)), vm((2, rq, deep // 2)),
         vm((zs, 2 * rq, width)), vm((zs, rq, width)), vm((zs - 1, rq, width)), vm((2, rq, width)),
         vm((zs, 2 * rq, 3 * local)), vm((zs, rq, 3 * local)), vm((zs - 1, rq, 3 * local)),
         vm((2, rq, 3 * local)),
@@ -1450,7 +1553,7 @@
             tokens, lengths, w_qkv, w_out, w_up, w_down, bias_q, bias_v, bias_out, bias_up,
             bias_down, gain_one, shift_one, gain_two, shift_two, cotangent,
         )
-    small = [bias_q, bias_v, bias_out, bias_down, gain_one, shift_one, gain_two, shift_two]
+    small = [bias_q, bias_v, gain_one, shift_one, bias_out, bias_down, gain_two, shift_two]
     out, gtok, gq, go, gu, gd, table = fused(
         tokens, lengths, w_qkv, w_out, w_up, w_down, small, bias_up, cotangent
     )
@@ -1463,7 +1566,7 @@
     )
     return (
         out, gtok, gq, go, gu, gd,
-        own[0], own[1], own[2], up, own[3], own[4], own[5], own[6], own[7],
+        own[0], own[1], own[4], up, own[5], own[2], own[3], own[6], own[7],
     )
 
 

time: 190 us -> 175 us (0.921)
  Pallas kernels: 179 us -> 163 us
    pallas_call x1, Pallas kernels: 179 us -> 163 us  [fused(): pl.pallas_call(fused_kernel, out_shape=(jax.ShapeDtypeStruct((rows, width...]
where the time goes in v3:
time: 175 us; the launch traced here: 174 us
  Pallas kernels  163 us (93%)
  local copies, waits for them, and re-layouts  10.2 us (6%)
    pallas_call x1, Pallas kernels, fused(): pl.pallas_call(fused_kernel, out_shape=(jax.ShapeDtypeStruct((rows, width...  163 us
    unnamed x16, local copies, waits for them, and re-layouts  6.4 us

profile of v3, /device:TPU:0, one launch (start us, length us, event | category | flops | bytes accessed | tf_op | source)
XLA Modules:
  0.0 174.5 jit_solution(7462038590512109792)
XLA Ops:
  0.7 0.8 stack.35
  1.5 0.7 tile.8
  2.1 0.1 broadcast_in_dim.27
  2.2 0.1 fusion.2
  2.3 0.1 tile.7
  2.5 0.6 pad_maximum_fusion.table
  3.1 162.8 %block.1 = (bf16[512,768]{1,0:T(8,128)(2,1)}, f32[512,768]{1,0:T(8,128)}, f32[48,2304]{1,0:T(8,128)}, f32[48,768]{1,0:T(8,128)}, f32[48,3072]{1,0:T(8,128)}, /*index=5*/f32[192,768]{1,0:T(8,128)}, f32[16,1,768]{2,1,0:T(1,128)}) custom-call(s32[1,6]{1,0:T(1,128)} %lengths.1, bf16[16,768]{1,0:T(8,128)(2,1)} %pad_maximum_fusion.table, ...), custom_call_target="tpu_custom_call" | custom-call | tf_op jit(solution)/shard_map/block/pallas_call | solution.py:1524
  165.9 0.0 copy-start
  165.9 0.9 fusion.15
  166.8 0.6 dynamic_slice.7
  167.4 0.6 fusion.7
  168.0 2.1 %copy.37 = bf16[512,768]{1,0:T(8,128)(2,1)} copy(bf16[512,768]{1,0:T(8,128)(2,1)} %get-tuple-element.54) | data formatting | bytes 1572864
  170.1 0.0 copy-done
  170.1 0.0 copy-start.3
  170.1 0.0 copy-start.4
  170.1 0.0 copy-start.2
  170.1 1.1 copy.38
  171.3 0.1 copy-done.3
  171.4 0.0 copy-start.1
  171.4 0.8 copy.39
  172.2 0.0 copy-done.4
  172.2 0.7 copy.40
  172.8 0.0 copy-done.2
  172.8 0.8 copy.41
  173.6 0.0 copy-done.1
  173.6 0.8 copy.42
  (5 shorter events, 0.0 us)
Async XLA Ops:
  165.9 4.2 %copy-start = (f32[512,768]{1,0:T(8,128)S(1)}, f32[512,768]{1,0:T(8,128)}, u32[]{:S(2)}) copy-start(f32[512,768]{1,0:T(8,128)} %get-tuple-element.55) | copy-start | bytes 4718596
  170.1 1.3 copy-start.3
  170.1 2.0 %copy-start.4 = (f32[48,768]{1,0:T(8,128)S(1)}, f32[48,768]{1,0:T(8,128)}, u32[]{:S(2)}) copy-start(f32[48,768]{1,0:T(8,128)} %get-tuple-element.57) | copy-start | bytes 442372
  170.1 2.7 %copy-start.2 = (f32[48,3072]{1,0:T(8,128)S(1)}, f32[48,3072]{1,0:T(8,128)}, u32[]{:S(2)}) copy-start(f32[48,3072]{1,0:T(8,128)} %get-tuple-element.58) | copy-start | bytes 1769476
  171.4 2.2 %copy-start.1 = (f32[192,768]{1,0:T(8,128)S(1)}, f32[192,768]{1,0:T(8,128)}, u32[]{:S(2)}) copy-start(f32[192,768]{1,0:T(8,128)} %get-tuple-element.59) | copy-start | bytes 1769476

commit v4 on v3

--- a/solution.py
+++ b/solution.py
@@ -1198,7 +1198,7 @@
         def _():
             early_rows.y_start()
 
-        @pl.when((t > 0) & (t <= early))
+        @pl.when((t > 0) & (t < early))
         def _():
             sum_e(t - 1).y_start()
 
@@ -1227,6 +1227,7 @@
             early_rows.next_start(1)
             sum_o.z_start()
             y_start_d(z)
+            sum_e(early - 1).y_start()
 
         @pl.when(k == 1)
         def _():
@@ -1234,19 +1235,20 @@
 
         @pl.when(k == 2)
         def _():
+            z_start_d(z)
             sum_e(0).z_start()
             sum_q(0).y_start()
 
         @pl.when(k == 3)
         def _():
-            sum_e(1).z_start()
             finish_o()
 
         @pl.when(k == 4)
         def _():
+            sum_e(early - 1).z_start()
             sum_u(2).y_start()
             sum_q(1).y_start()
-            z_start_d(z)
+            finish_d()
 
         @pl.when(k == 5)
         def _():
@@ -1348,7 +1350,6 @@
     late_rows.z_start()
     sum_u(2).z_start()
     sum_q(1).z_start()
-    finish_d()
     sum_u(3).z_start()
 
     def fall(i):
@@ -1542,6 +1543,23 @@
     )(lengths, table, tokens, cotangent, w_qkv, w_out, w_up, w_down)
 
 
+def closing_kernel(*refs):
+    given, table, taken = refs[:6], refs[6], refs[7:]
+    d = lax.axis_index("dp")
+    for source, there in zip(given, taken[:6]):
+        there[...] = source[...]
+    own, up = taken[6:14], taken[14]
+    width = table.shape[2]
+    rq, rd = own[0].shape[1], up.shape[1]
+    rows = jnp.concatenate([table[i] for i in range(8)], axis=0)
+    moved = pltpu.roll(rows, lax.rem(width - d * rq, width), 1)
+    for i in range(8):
+        own[i][...] = moved[i : i + 1, :rq]
+    row = jnp.broadcast_to(table[BIAS_UP + lax.div(d * rd, width)], (8, width))
+    moved = pltpu.roll(row, lax.rem(width - lax.rem(d * rd, width), width), 1)
+    up[...] = moved[0:1, :rd]
+
+
 def per_device(
     tokens, lengths, w_qkv, w_out, w_up, w_down, bias_q, bias_v, bias_out, bias_up, bias_down,
     gain_one, shift_one, gain_two, shift_two, cotangent,
@@ -1554,16 +1572,20 @@
             bias_down, gain_one, shift_one, gain_two, shift_two, cotangent,
         )
     small = [bias_q, bias_v, gain_one, shift_one, bias_out, bias_down, gain_two, shift_two]
-    out, gtok, gq, go, gu, gd, table = fused(
+    results = fused(
         tokens, lengths, w_qkv, w_out, w_up, w_down, small, bias_up, cotangent
     )
-    d = lax.axis_index("dp")
-    width = tokens.shape[1]
     rq, rd = w_qkv.shape[0], w_down.shape[0]
-    own = lax.dynamic_slice_in_dim(table[:8, 0], d * rq, rq, axis=1)
-    up = lax.dynamic_slice_in_dim(
-        table[8:].reshape((TABLE - 8) * width), d * rd, rd, axis=0
-    )
+    here = pl.BlockSpec(memory_space=pltpu.VMEM)
+    out, gtok, gq, go, gu, gd, *own, up = pl.pallas_call(
+        closing_kernel,
+        out_shape=tuple(jax.ShapeDtypeStruct(a.shape, a.dtype) for a in results[:6])
+        + (jax.ShapeDtypeStruct((1, rq), F32),) * 8 + (jax.ShapeDtypeStruct((1, rd), F32),),
+        in_specs=[here] * 7,
+        out_specs=[here] * 15,
+        name="closing",
+    )(*results)
+    own, up = [piece[0] for piece in own], up[0]
     return (
         out, gtok, gq, go, gu, gd,
         own[0], own[1], own[4], up, own[5], own[2], own[3], own[6], own[7],

time: 175 us -> 167 us (0.954)
  local copies, waits for them, and re-layouts: 10.2 us -> 1.66 us
    unnamed x16 -> x0, local copies, waits for them, and re-layouts: 6.4 us -> none
    pallas_call x0 -> x1, Pallas kernels: none -> 4.28 us  [per_device(): pl.pallas_call(closing_kernel, out_shape=tuple((jax.ShapeDtypeStruct(a.sh...]
    pallas_call x1, Pallas kernels: 163 us -> 160 us  [fused(): pl.pallas_call(fused_kernel, out_shape=(jax.ShapeDtypeStruct((rows, width...]
where the time goes in v4:
time: 167 us
  Pallas kernels  164 us (98%)
    pallas_call x1, Pallas kernels, fused(): pl.pallas_call(fused_kernel, out_shape=(jax.ShapeDtypeStruct((rows, width...  160 us
    pallas_call x1, Pallas kernels, per_device(): pl.pallas_call(closing_kernel, out_shape=tuple((jax.ShapeDtypeStruct(a.sh...  4.28 us

profile of v4, /device:TPU:0, one launch (start us, length us, event | category | flops | bytes accessed | tf_op | source)
XLA Modules:
  0.0 167.1 jit_solution(4871387064944224638)
XLA Ops:
  0.7 0.8 stack.35
  1.5 0.7 tile.8
  2.1 0.1 broadcast_in_dim.27
  2.2 0.1 fusion.2
  2.3 0.1 tile.7
  2.5 0.6 pad_maximum_fusion.table
  3.1 159.6 %block.1 = (bf16[512,768]{1,0:T(8,128)(2,1)}, f32[512,768]{1,0:T(8,128)}, f32[48,2304]{1,0:T(8,128)}, f32[48,768]{1,0:T(8,128)}, f32[48,3072]{1,0:T(8,128)}, /*index=5*/f32[192,768]{1,0:T(8,128)}, f32[16,1,768]{2,1,0:T(1,128)}) custom-call(s32[1,6]{1,0:T(1,128)} %lengths.1, bf16[16,768]{1,0:T(8,128)(2,1)} %pad_maximum_fusion.table, ...), custom_call_target="tpu_custom_call" | custom-call | tf_op jit(solution)/shard_map/block/pallas_call | solution.py:1525
  162.7 4.3 %closing.1 = (bf16[512,768]{1,0:T(8,128)(2,1)}, f32[512,768]{1,0:T(8,128)}, f32[48,2304]{1,0:T(8,128)}, f32[48,768]{1,0:T(8,128)}, f32[48,3072]{1,0:T(8,128)}, /...) custom-call(bf16[512,768]{1,0:T(8,128)(2,1)} %get-tuple-element.37.r, ...), custom_call_target="tpu_custom_call" | custom-call | tf_op jit(solution)/shard_map/closing/pallas_call | solution.py:1580
  (5 shorter events, 0.0 us)

commit v5 on v4

--- a/solution.py
+++ b/solution.py
@@ -1028,6 +1028,14 @@
         def _():
             x_start_d(turn(2, z))
 
+    def weigh_down(t):
+        def part(m):
+            at = pl.ds(pl.multiple_of(m * 2 * rd, 2 * rd), 2 * rd)
+            gwd[t, at, :] = mul(hidden_t[at, :], gout[...]).astype(BF)
+
+        loop(2, part)
+        sib_start_d(t)
+
     def feed(i):
         t = turn(i, z)
         gather_u(i).finish()
@@ -1042,8 +1050,11 @@
         hidden_t[...] = rounded.T
         slope[:, at] = bend.astype(BF)
         pass_up(i * 2)
-        gwd[t] = mul(hidden_t[...], gout[...]).astype(BF)
-        sib_start_d(t)
+
+        @pl.when(i < tiles - 1)
+        def _():
+            weigh_down(t)
+
         pass_up(i * 2 + 1)
 
     loop(tiles, feed)
@@ -1058,14 +1069,13 @@
         gvec[BIAS_UP + t] = column_sum(grad.astype(F32))
 
     loop(tiles, slopes_back)
-    y_start_d(turn(1, z))
-    z_start_d(turn(0, z))
 
     def grow(i):
         at = pl.ds(pl.multiple_of(i * side, side), side)
         gtok[at, :] = mul_nt(slope[at, :], flat(wu[...]))
 
     loop(rows // side, grow)
+    y_start_d(turn(1, z))
 
     for row in (BIAS_Q, BIAS_V, BIAS_OUT, BIAS_DOWN, GAIN_1, SHIFT_1, GAIN_2, SHIFT_2):
         gvec[row] = jnp.zeros((1, width), F32)
@@ -1156,14 +1166,16 @@
     )
     send_gmix(0).start()
     keep_gmix.start()
+    early_rows.z_start()
+    weigh_down(z)
+
+    gather_o.sent()
+
+    wo[...] = mul(mixed_t[...], gattn[...]).astype(BF).reshape(zs, 4 * rq, width)
     x_start_d(z)
     for p in range(1, pairs):
         send_gmix(p).start()
-    early_rows.z_start()
-
-    gather_o.sent()
-
-    wo[...] = mul(mixed_t[...], gattn[...]).astype(BF).reshape(zs, 4 * rq, width)
+    z_start_d(turn(0, z))
     y_start_d(turn(2, z))
     z_start_d(turn(1, z))
     for t in range(tiles):
@@ -1576,13 +1588,19 @@
         tokens, lengths, w_qkv, w_out, w_up, w_down, small, bias_up, cotangent
     )
     rq, rd = w_qkv.shape[0], w_down.shape[0]
-    here = pl.BlockSpec(memory_space=pltpu.VMEM)
+    steps = 2
+
+    def whole(shape):
+        return pl.BlockSpec(shape, lambda i: (0,) * len(shape))
+
+    cut = [pl.BlockSpec((a.shape[0] // steps, a.shape[1]), lambda i: (i, 0)) for a in results[:6]]
     out, gtok, gq, go, gu, gd, *own, up = pl.pallas_call(
         closing_kernel,
+        grid=(steps,),
         out_shape=tuple(jax.ShapeDtypeStruct(a.shape, a.dtype) for a in results[:6])
         + (jax.ShapeDtypeStruct((1, rq), F32),) * 8 + (jax.ShapeDtypeStruct((1, rd), F32),),
-        in_specs=[here] * 7,
-        out_specs=[here] * 15,
+        in_specs=cut + [whole(results[6].shape)],
+        out_specs=cut + [whole((1, rq))] * 8 + [whole((1, rd))],
         name="closing",
     )(*results)
     own, up = [piece[0] for piece in own], up[0]

time: 167 us -> 166 us (level)
  Pallas kernels: 164 us -> 162 us
where the time goes in v5:
time: 166 us
  Pallas kernels  162 us (98%)
    pallas_call x1, Pallas kernels, fused(): pl.pallas_call(fused_kernel, out_shape=(jax.ShapeDtypeStruct((rows, width...  158 us
    pallas_call x1, Pallas kernels, per_device(): pl.pallas_call(closing_kernel, grid=(steps,), out_shape=tuple((jax.ShapeD...  3.92 us

profile of v5, /device:TPU:0, one launch (start us, length us, event | category | flops | bytes accessed | tf_op | source)
XLA Modules:
  0.0 165.6 jit_solution(16032831947111487647)
XLA Ops:
  0.7 0.8 stack.35
  1.5 0.7 tile.8
  2.1 0.1 broadcast_in_dim.27
  2.2 0.1 fusion.2
  2.3 0.1 tile.7
  2.5 0.6 pad_maximum_fusion.table
  3.1 158.4 %block.1 = (bf16[512,768]{1,0:T(8,128)(2,1)}, f32[512,768]{1,0:T(8,128)}, f32[48,2304]{1,0:T(8,128)}, f32[48,768]{1,0:T(8,128)}, f32[48,3072]{1,0:T(8,128)}, /*index=5*/f32[192,768]{1,0:T(8,128)}, f32[16,1,768]{2,1,0:T(1,128)}) custom-call(s32[1,6]{1,0:T(1,128)} %lengths.1, bf16[16,768]{1,0:T(8,128)(2,1)} %pad_maximum_fusion.table, ...), custom_call_target="tpu_custom_call" | custom-call | tf_op jit(solution)/shard_map/block/pallas_call | solution.py:1537
  161.5 3.9 %closing.1 = (bf16[512,768]{1,0:T(8,128)(2,1)}, f32[512,768]{1,0:T(8,128)}, f32[48,2304]{1,0:T(8,128)}, f32[48,768]{1,0:T(8,128)}, f32[48,3072]{1,0:T(8,128)}, /...) custom-call(bf16[512,768]{1,0:T(8,128)(2,1)} %get-tuple-element.37.r, ...), custom_call_target="tpu_custom_call" | custom-call | tf_op jit(solution)/shard_map/closing/pallas_call | solution.py:1597
  (5 shorter events, 0.0 us)

commit v6 on v5

--- a/solution.py
+++ b/solution.py
@@ -1058,7 +1058,6 @@
         pass_up(i * 2 + 1)
 
     loop(tiles, feed)
-    y_start_d(turn(0, z))
     for i in range(cuts):
         gather_d(i).finish()
 
@@ -1069,6 +1068,7 @@
         gvec[BIAS_UP + t] = column_sum(grad.astype(F32))
 
     loop(tiles, slopes_back)
+    y_start_d(turn(0, z))
 
     def grow(i):
         at = pl.ds(pl.multiple_of(i * side, side), side)

time: 166 us -> 166 us (level)
  no operation moved by 1% of the time
where the time goes in v6:
time: 166 us
  Pallas kernels  162 us (98%)
    pallas_call x1, Pallas kernels, fused(): pl.pallas_call(fused_kernel, out_shape=(jax.ShapeDtypeStruct((rows, width...  158 us
    pallas_call x1, Pallas kernels, per_device(): pl.pallas_call(closing_kernel, grid=(steps,), out_shape=tuple((jax.ShapeD...  3.92 us

profile of v6, /device:TPU:0, one launch (start us, length us, event | category | flops | bytes accessed | tf_op | source)
XLA Modules:
  0.0 165.6 jit_solution(1364618443074801176)
XLA Ops:
  0.7 0.8 stack.35
  1.5 0.7 tile.8
  2.1 0.1 broadcast_in_dim.27
  2.2 0.1 fusion.2
  2.3 0.1 tile.7
  2.5 0.6 pad_maximum_fusion.table
  3.1 158.4 %block.1 = (bf16[512,768]{1,0:T(8,128)(2,1)}, f32[512,768]{1,0:T(8,128)}, f32[48,2304]{1,0:T(8,128)}, f32[48,768]{1,0:T(8,128)}, f32[48,3072]{1,0:T(8,128)}, /*index=5*/f32[192,768]{1,0:T(8,128)}, f32[16,1,768]{2,1,0:T(1,128)}) custom-call(s32[1,6]{1,0:T(1,128)} %lengths.1, bf16[16,768]{1,0:T(8,128)(2,1)} %pad_maximum_fusion.table, ...), custom_call_target="tpu_custom_call" | custom-call | tf_op jit(solution)/shard_map/block/pallas_call | solution.py:1537
  161.5 3.9 %closing.1 = (bf16[512,768]{1,0:T(8,128)(2,1)}, f32[512,768]{1,0:T(8,128)}, f32[48,2304]{1,0:T(8,128)}, f32[48,768]{1,0:T(8,128)}, f32[48,3072]{1,0:T(8,128)}, /...) custom-call(bf16[512,768]{1,0:T(8,128)(2,1)} %get-tuple-element.37.r, ...), custom_call_target="tpu_custom_call" | custom-call | tf_op jit(solution)/shard_map/closing/pallas_call | solution.py:1597
  (5 shorter events, 0.0 us)
